TPU v7x, 256 devices: a whole 4x4x8 slice. The times are simulated.
256 devices in a mesh: cell: 16 (over x, z_lo, core), gene: 16 (over y, z_hi).
Axes of the slice: x: 4, y: 4, z: 8 (z_hi: 4, z_lo: 2; z = z_hi * 2 + z_lo), core: 2. Of those that a mesh axis runs over, the one named last changes fastest.
Arguments:
- query_rows: bfloat16 [16, 2048, 1536], P('cell', 'gene'), may hold values from -1.5 to 1.5
- key_rows: bfloat16 [16, 2048, 1536], P('cell', 'gene'), may hold values from -1.5 to 1.5
- value_rows: bfloat16 [16, 2048, 1536], P('cell', 'gene'), may hold values from -6 to 6
- output_rows: bfloat16 [16, 2048, 1536], P('cell', 'gene'), may hold values from -6 to 6
- output_grad: bfloat16 [16, 2048, 1536], P('cell', 'gene'), may hold values from -6 to 6
- row_lse: float32 [16, 2048, 12], P('cell', 'gene'), may hold values from 3 to 6
- block_bias: float32 [16, 12, 16], replicated, may hold values from -1.5 to 1.5
- block_index: int32 [16, 16], replicated, may hold values from 0 to 15, each once within a row
- block_count: int32 [16], replicated, may hold values from 1 to 16, 128 in all
Outputs:
- query_grad: bfloat16 [16, 2048, 1536], P('cell', 'gene')
- key_grad: bfloat16 [16, 2048, 1536], P('cell', 'gene')
- value_grad: bfloat16 [16, 2048, 1536], P('cell', 'gene')
- bias_grad: float32 [16, 12, 16], P('gene', None, 'cell')
Inputs may be any that keep to these rules, and one draw needn't show every extreme that they name: Each row of block_index lists every key block once; its first block_count entries are the listed ones, and one row block lists all 16. `block_count`: one row block has 16 listed key blocks.
All inputs are finite; a program needn't handle non-finite values.
Results may differ from a plain program's by a relative error of at most 0.0049.
Values may be sent and summed in bfloat16 or wider, within the bound.
A program may use at most 128 MiB of HBM per device.

v0:
```python
import math

import jax
import jax.numpy as jnp
from jax import lax
from jax.sharding import PartitionSpec as P

BLOCK = 128


def in_one_piece(arrays, axis, dim, along):
    ends, at = ([], 0)
    for a in arrays[:-1]:
        at += a.shape[along]
        ends.append(at)
    both = jnp.concatenate(arrays, axis=along)
    return tuple(jnp.split(lax.all_gather(both, axis, axis=dim, tiled=True), ends, axis=along))


def pair_tables(block_bias, block_index, block_count):
    block_total = block_bias.shape[0]
    columns = jnp.arange(block_total, dtype=jnp.int32)
    slot_live = jnp.arange(block_index.shape[1], dtype=jnp.int32)[None, :] < block_count[:, None]
    listed = ((block_index[:, :, None] == columns[None, None, :]) & slot_live[:, :, None]).astype(
        jnp.float32
    )
    pair_bias = jnp.einsum("ihs,isj->hij", block_bias, listed, precision=lax.Precision.HIGHEST)
    pair_mask = jnp.sum(listed, axis=1)
    return (listed, pair_bias, pair_mask)


def block_onehot(positions, block_total):
    return (
        positions[:, None] // BLOCK == jnp.arange(block_total, dtype=jnp.int32)[None, :]
    ).astype(jnp.float32)


def pair_slice(table, row_hot, col_hot):
    picked = jnp.einsum("ri,hij->hrj", row_hot, table, precision=lax.Precision.HIGHEST)
    return jnp.einsum("hrj,kj->hrk", picked, col_hot, precision=lax.Precision.HIGHEST)


def split_heads(array, head_count):
    return array.reshape(array.shape[0], array.shape[1], head_count, -1)


def score_terms(
    query_heads,
    grad_heads,
    lse_rows,
    delta_rows,
    key_heads,
    value_heads,
    pair_part,
    mask_part,
    score_scale,
):
    scores = (
        jnp.einsum("crhd,ckhd->chrk", query_heads, key_heads, preferred_element_type=jnp.float32)
        * score_scale
    )
    scores = scores + pair_part[None]
    weights = jnp.where(mask_part[None, None] > 0.5, jnp.exp(scores - lse_rows[..., None]), 0.0)
    weight_grads = jnp.einsum(
        "crhd,ckhd->chrk", grad_heads, value_heads, preferred_element_type=jnp.float32
    )
    score_grads = weights * (weight_grads - delta_rows[..., None])
    return (weights, score_grads)


def over_blocks(running, pieces, work):
    length = pieces[0].shape[1]

    def step_block(step_index, state):
        offset = step_index * BLOCK
        sliced = tuple((lax.dynamic_slice_in_dim(piece, offset, BLOCK, 1) for piece in pieces))
        return work(state, sliced, offset)

    return lax.fori_loop(0, length // BLOCK, step_block, running)


def shards(
    query_rows,
    key_rows,
    value_rows,
    output_rows,
    output_grad,
    row_lse,
    block_bias,
    block_index,
    block_count,
):
    cell_count, row_count, row_width = query_rows.shape
    head_count = row_lse.shape[2]
    head_size = row_width // head_count
    block_total = block_bias.shape[0]
    my_blocks = row_count // BLOCK
    first_row = lax.axis_index("gene") * row_count
    score_scale = 1.0 / math.sqrt(head_size)
    listed, pair_bias, pair_mask = pair_tables(block_bias, block_index, block_count)
    mask_table = pair_mask[None]
    row_hot = block_onehot(first_row + jnp.arange(row_count, dtype=jnp.int32), block_total)
    query_heads = split_heads(query_rows, head_count)
    grad_heads = split_heads(output_grad, head_count)
    key_heads = split_heads(key_rows, head_count)
    value_heads = split_heads(value_rows, head_count)
    row_delta = jnp.sum(
        grad_heads.astype(jnp.float32) * split_heads(output_rows, head_count).astype(jnp.float32),
        axis=-1,
    )
    lse_mine = jnp.transpose(row_lse, (0, 2, 1))
    delta_mine = jnp.transpose(row_delta, (0, 2, 1))
    all_lse, all_delta = (
        lax.all_gather(row_lse, "gene", axis=1, tiled=True),
        lax.all_gather(row_delta, "gene", axis=1, tiled=True),
    )

    def query_work(running, pieces, begin_at):
        key_part, value_part = pieces
        part_len = key_part.shape[1]
        col_hot = block_onehot(begin_at + jnp.arange(part_len, dtype=jnp.int32), block_total)
        mask_part = pair_slice(mask_table, row_hot, col_hot)[0]

        def query_compute(state):
            grad_query, bias_sums = state
            pair_part = pair_slice(pair_bias, row_hot, col_hot)
            part_keys = split_heads(key_part, head_count)
            weights, score_grads = score_terms(
                query_heads,
                grad_heads,
                lse_mine,
                delta_mine,
                part_keys,
                split_heads(value_part, head_count),
                pair_part,
                mask_part,
                score_scale,
            )
            grads_low = score_grads.astype(jnp.bfloat16)
            grad_query = grad_query + jnp.einsum(
                "chrk,ckhd->crhd", grads_low, part_keys, preferred_element_type=jnp.float32
            )
            summed = (
                jnp.sum(score_grads, axis=0)
                .reshape(head_count, my_blocks, BLOCK, part_len)
                .sum(axis=2)
            )
            bias_sums = bias_sums + jnp.einsum(
                "hik,kj->hij", summed, col_hot, precision=lax.Precision.HIGHEST
            )
            return (grad_query, bias_sums)

        return lax.cond(jnp.sum(mask_part) > 0.5, query_compute, lambda state: state, running)

    def owner_work(running, pieces, begin_at):
        query_part, grad_part = pieces
        part_len = query_part.shape[1]
        part_hot = block_onehot(begin_at + jnp.arange(part_len, dtype=jnp.int32), block_total)
        mask_part = pair_slice(mask_table, part_hot, row_hot)[0]

        def owner_compute(state):
            grad_key, grad_value = state
            pair_part = pair_slice(pair_bias, part_hot, row_hot)
            lse_part = jnp.transpose(
                lax.dynamic_slice_in_dim(all_lse, begin_at, part_len, 1), (0, 2, 1)
            )
            delta_part = jnp.transpose(
                lax.dynamic_slice_in_dim(all_delta, begin_at, part_len, 1), (0, 2, 1)
            )
            part_queries = split_heads(query_part, head_count)
            part_grads = split_heads(grad_part, head_count)
            weights, score_grads = score_terms(
                part_queries,
                part_grads,
                lse_part,
                delta_part,
                key_heads,
                value_heads,
                pair_part,
                mask_part,
                score_scale,
            )
            grad_value = grad_value + jnp.einsum(
                "chnk,cnhd->ckhd",
                weights.astype(jnp.bfloat16),
                part_grads,
                preferred_element_type=jnp.float32,
            )
            grad_key = grad_key + jnp.einsum(
                "chnk,cnhd->ckhd",
                score_grads.astype(jnp.bfloat16),
                part_queries,
                preferred_element_type=jnp.float32,
            )
            return (grad_key, grad_value)

        return lax.cond(jnp.sum(mask_part) > 0.5, owner_compute, lambda state: state, running)

    zero_heads = jnp.zeros((cell_count, row_count, head_count, head_size), jnp.float32)
    zero_sums = jnp.zeros((head_count, my_blocks, block_total), jnp.float32)
    grad_query, bias_sums = over_blocks(
        (zero_heads, zero_sums),
        (
            lax.all_gather(key_rows, "gene", axis=1, tiled=True),
            lax.all_gather(value_rows, "gene", axis=1, tiled=True),
        ),
        query_work,
    )
    grad_key, grad_value = over_blocks(
        (zero_heads, zero_heads), in_one_piece((query_rows, output_grad), "gene", 1, 0), owner_work
    )
    flat_shape = (cell_count, row_count, row_width)
    query_grad = (grad_query * score_scale).astype(jnp.bfloat16).reshape(flat_shape)
    key_grad = (grad_key * score_scale).astype(jnp.bfloat16).reshape(flat_shape)
    value_grad = grad_value.astype(jnp.bfloat16).reshape(flat_shape)
    listed_mine = lax.dynamic_slice_in_dim(listed, lax.axis_index("gene") * my_blocks, my_blocks, 0)
    bias_terms = jnp.einsum("hij,isj->ihs", bias_sums, listed_mine, precision=lax.Precision.HIGHEST)
    bias_grad = lax.psum_scatter(bias_terms, "cell", scatter_dimension=2, tiled=True)
    return (query_grad, key_grad, value_grad, bias_grad)


def solution(mesh):
    in_specs = (
        P("cell", "gene", None),
        P("cell", "gene", None),
        P("cell", "gene", None),
        P("cell", "gene", None),
        P("cell", "gene", None),
        P("cell", "gene", None),
        P(),
        P(),
        P(),
    )
    out_specs = (
        P("cell", "gene", None),
        P("cell", "gene", None),
        P("cell", "gene", None),
        P("gene", None, "cell"),
    )
    return jax.shard_map(shards, mesh=mesh, in_specs=in_specs, out_specs=out_specs, check_vma=False)
```

profile of v0, /device:TPU:131, one launch (start us, length us, event | category | flops | bytes accessed | tf_op | source)
XLA Modules:
  0.0 516.4 jit_solution(10261313486045301067)
XLA Ops:
  19.5 38.0 %all-gather = f32[2048,12]{0,1:T(8,128)} all-gather(f32[128,12]{0,1:T(8,128)S(1)} %fusion.47), channel_id=2, replica_groups=mesh['cell'=16,'gene'=16] {'gene'}, dimensions={0}, use_global_device_ids=true | all-gather | bytes 104448 | tf_op jit(solution)/shard_map/all_gather | solution.py:115
  57.5 45.0 %all_gather.18 = f32[1,2048,12]{1,2,0:T(8,128)} all-gather(f32[1,128,12]{1,2,0:T(8,128)S(1)} %copy.117), channel_id=1, replica_groups=mesh['cell'=16,'gene'=16] {'gene'}, dimensions={1}, use_global_device_ids=true | all-gather | bytes 104448 | tf_op jit(solution)/shard_map/all_gather | solution.py:114
  103.5 13.0 %all-gather.5.cloned.1.call-done = bf16[1,2048,1536]{1,2,0:T(8,128)(2,1)} async-done(((bf16[1,128,1536]{1,2,0:T(8,128)(2,1)}), bf16[1,2048,1536]{1,2,0:T(8,128)(2,1)}) %all-gather.5.cloned.1.call-update) | async-done | bytes 6291472 | tf_op jit(solution)/shard_map/all_gather | solution.py:204
  116.5 102.7 %all-gather.7.cloned.1.call-done = bf16[1,2048,1536]{1,2,0:T(8,128)(2,1)} async-done(((bf16[1,128,1536]{1,2,0:T(8,128)(2,1)}), bf16[1,2048,1536]{1,2,0:T(8,128)(2,1)}) %all-gather.7.cloned.1.call-update) | async-done | bytes 6291472 | tf_op jit(solution)/shard_map/all_gather | solution.py:205
  219.3 46.0 %while.36 = (s32[]{:T(128)}, f32[1,128,12,128]{1,3,2,0:T(8,128)S(1)}, f32[12,1,16]{2,0,1:T(8,128)S(1)}, f32[16,128]{1,0:T(8,128)S(1)}, bf16[1,2048,1536]{1,2,0:T...) while((s32[]{:T(128)}, ...), condition=%wide.region_7.8_spmd.clone, body=%wide.region_2.7_spmd.clone.sunk | while | flops 198716096 | bytes 9625445 | solution.py:79
  228.7 5.2 %conditional.6 = ((f32[1,128,12,128]{1,3,2,0:T(8,128)S(1)}, f32[12,1,16]{2,0,1:T(8,128)S(1)})) conditional(s32[]{:T(128)} %convert_element_type.152, (f32[1,128,12,128]{1,3,2,0:T(8,128)S(1)}, f32[12,1,16]{2,0,1:T(8,128)S(1)}) %tuple.150, (s32[]{:T(128)}, bf16[1,2048,1536]{1,2,0:T(8,128)(2,1)}, f32[128,128]{0,1:T(8,128)S(1)}, ...), branch_computations={%region_4.4_spmd, %region_5.6_spmd} | conditional | flops 195541696 | bytes 9532990 | solution.py:153
  240.1 5.3 %conditional.6 = ((f32[1,128,12,128]{1,3,2,0:T(8,128)S(1)}, f32[12,1,16]{2,0,1:T(8,128)S(1)})) conditional(s32[]{:T(128)} %convert_element_type.152, (f32[1,128,12,128]{1,3,2,0:T(8,128)S(1)}, f32[12,1,16]{2,0,1:T(8,128)S(1)}) %tuple.150, (s32[]{:T(128)}, bf16[1,2048,1536]{1,2,0:T(8,128)(2,1)}, f32[128,128]{0,1:T(8,128)S(1)}, ...), branch_computations={%region_4.4_spmd, %region_5.6_spmd} | conditional | flops 195541696 | bytes 9532990 | solution.py:153
  251.7 5.2 %conditional.6 = ((f32[1,128,12,128]{1,3,2,0:T(8,128)S(1)}, f32[12,1,16]{2,0,1:T(8,128)S(1)})) conditional(s32[]{:T(128)} %convert_element_type.152, (f32[1,128,12,128]{1,3,2,0:T(8,128)S(1)}, f32[12,1,16]{2,0,1:T(8,128)S(1)}) %tuple.150, (s32[]{:T(128)}, bf16[1,2048,1536]{1,2,0:T(8,128)(2,1)}, f32[128,128]{0,1:T(8,128)S(1)}, ...), branch_computations={%region_4.4_spmd, %region_5.6_spmd} | conditional | flops 195541696 | bytes 9532990 | solution.py:153
  260.0 5.2 %conditional.6 = ((f32[1,128,12,128]{1,3,2,0:T(8,128)S(1)}, f32[12,1,16]{2,0,1:T(8,128)S(1)})) conditional(s32[]{:T(128)} %convert_element_type.152, (f32[1,128,12,128]{1,3,2,0:T(8,128)S(1)}, f32[12,1,16]{2,0,1:T(8,128)S(1)}) %tuple.150, (s32[]{:T(128)}, bf16[1,2048,1536]{1,2,0:T(8,128)(2,1)}, f32[128,128]{0,1:T(8,128)S(1)}, ...), branch_computations={%region_4.4_spmd, %region_5.6_spmd} | conditional | flops 195541696 | bytes 9532990 | solution.py:153
  267.1 24.7 %all-reduce = f32[1,12,16]{1,0,2:T(1,128)S(1)} all-reduce(f32[1,12,16]{1,0,2:T(1,128)S(1)} %bitcast.168), channel_id=3, replica_groups=mesh['cell'=16,'gene'=16] {'cell'}, use_global_device_ids=true, to_apply=%region_13.14.clone | all-reduce | flops 192 | bytes 1536
  292.9 97.8 %all-gather.9.cloned.1.call-done = bf16[2,2048,1536]{1,2,0:T(8,128)(2,1)} async-done(((bf16[2,128,1536]{1,2,0:T(8,128)(2,1)}), bf16[2,2048,1536]{1,2,0:T(8,128)(2,1)}) %all-gather.9.cloned.1.call-update) | async-done | bytes 12582928 | tf_op jit(solution)/shard_map/all_gather | solution.py:17
  390.7 10.6 %fusion.61 = (bf16[1,2048,1536]{1,2,0:T(8,128)(2,1)}, bf16[1,2048,1536]{1,2,0:T(8,128)(2,1)}) fusion(bf16[2,2048,1536]{1,2,0:T(8,128)(2,1)} %all-gather.9.cloned.1.call-done), kind=kLoop, calls=%fused_computation.101 | loop fusion | bytes 25165824 | tf_op jit(solution)/shard_map/split | solution.py:17
  401.4 106.5 %while.37 = (s32[]{:T(128)}, f32[1,128,12,128]{1,3,2,0:T(8,128)S(1)}, f32[1,128,12,128]{1,3,2,0:T(8,128)S(1)}, f32[1,16,16]{2,1,0:T(8,128)S(1)}, bf16[1,2048,153...) while((s32[]{:T(128)}, ...), condition=%wide.region_12.13_spmd.clone, body=%wide.region_8.0_spmd.clone.sunk | while | flops 249348096 | bytes 11472745 | solution.py:79
  405.0 7.1 %conditional.7 = ((f32[1,128,12,128]{1,3,2,0:T(8,128)S(1)}, f32[1,128,12,128]{1,3,2,0:T(8,128)S(1)})) conditional(s32[]{:T(128)} %convert_element_type.155, (f32[1,128,12,128]{1,3,2,0:T(8,128)S(1)}, f32[1,128,12,128]{1,3,2,0:T(8,128)S(1)}) %tuple.155, (s32[]{:T(128)}, bf16[1,2048,1536]{1,2,0:T(8,128)(2,1)}, f32[128,128]{1,0:T(8,128)S(1)}, ...), branch_computations={%region_10.10_spmd, %region_11.11_spmd} | conditional | flops 245776384 | bytes 11370562 | solution.py:197
  415.6 7.1 %conditional.7 = ((f32[1,128,12,128]{1,3,2,0:T(8,128)S(1)}, f32[1,128,12,128]{1,3,2,0:T(8,128)S(1)})) conditional(s32[]{:T(128)} %convert_element_type.155, (f32[1,128,12,128]{1,3,2,0:T(8,128)S(1)}, f32[1,128,12,128]{1,3,2,0:T(8,128)S(1)}) %tuple.155, (s32[]{:T(128)}, bf16[1,2048,1536]{1,2,0:T(8,128)(2,1)}, f32[128,128]{1,0:T(8,128)S(1)}, ...), branch_computations={%region_10.10_spmd, %region_11.11_spmd} | conditional | flops 245776384 | bytes 11370562 | solution.py:197
  424.5 7.1 %conditional.7 = ((f32[1,128,12,128]{1,3,2,0:T(8,128)S(1)}, f32[1,128,12,128]{1,3,2,0:T(8,128)S(1)})) conditional(s32[]{:T(128)} %convert_element_type.155, (f32[1,128,12,128]{1,3,2,0:T(8,128)S(1)}, f32[1,128,12,128]{1,3,2,0:T(8,128)S(1)}) %tuple.155, (s32[]{:T(128)}, bf16[1,2048,1536]{1,2,0:T(8,128)(2,1)}, f32[128,128]{1,0:T(8,128)S(1)}, ...), branch_computations={%region_10.10_spmd, %region_11.11_spmd} | conditional | flops 245776384 | bytes 11370562 | solution.py:197
  435.2 7.1 %conditional.7 = ((f32[1,128,12,128]{1,3,2,0:T(8,128)S(1)}, f32[1,128,12,128]{1,3,2,0:T(8,128)S(1)})) conditional(s32[]{:T(128)} %convert_element_type.155, (f32[1,128,12,128]{1,3,2,0:T(8,128)S(1)}, f32[1,128,12,128]{1,3,2,0:T(8,128)S(1)}) %tuple.155, (s32[]{:T(128)}, bf16[1,2048,1536]{1,2,0:T(8,128)(2,1)}, f32[128,128]{1,0:T(8,128)S(1)}, ...), branch_computations={%region_10.10_spmd, %region_11.11_spmd} | conditional | flops 245776384 | bytes 11370562 | solution.py:197
  444.0 7.1 %conditional.7 = ((f32[1,128,12,128]{1,3,2,0:T(8,128)S(1)}, f32[1,128,12,128]{1,3,2,0:T(8,128)S(1)})) conditional(s32[]{:T(128)} %convert_element_type.155, (f32[1,128,12,128]{1,3,2,0:T(8,128)S(1)}, f32[1,128,12,128]{1,3,2,0:T(8,128)S(1)}) %tuple.155, (s32[]{:T(128)}, bf16[1,2048,1536]{1,2,0:T(8,128)(2,1)}, f32[128,128]{1,0:T(8,128)S(1)}, ...), branch_computations={%region_10.10_spmd, %region_11.11_spmd} | conditional | flops 245776384 | bytes 11370562 | solution.py:197
  452.9 7.1 %conditional.7 = ((f32[1,128,12,128]{1,3,2,0:T(8,128)S(1)}, f32[1,128,12,128]{1,3,2,0:T(8,128)S(1)})) conditional(s32[]{:T(128)} %convert_element_type.155, (f32[1,128,12,128]{1,3,2,0:T(8,128)S(1)}, f32[1,128,12,128]{1,3,2,0:T(8,128)S(1)}) %tuple.155, (s32[]{:T(128)}, bf16[1,2048,1536]{1,2,0:T(8,128)(2,1)}, f32[128,128]{1,0:T(8,128)S(1)}, ...), branch_computations={%region_10.10_spmd, %region_11.11_spmd} | conditional | flops 245776384 | bytes 11370562 | solution.py:197
  461.8 7.1 %conditional.7 = ((f32[1,128,12,128]{1,3,2,0:T(8,128)S(1)}, f32[1,128,12,128]{1,3,2,0:T(8,128)S(1)})) conditional(s32[]{:T(128)} %convert_element_type.155, (f32[1,128,12,128]{1,3,2,0:T(8,128)S(1)}, f32[1,128,12,128]{1,3,2,0:T(8,128)S(1)}) %tuple.155, (s32[]{:T(128)}, bf16[1,2048,1536]{1,2,0:T(8,128)(2,1)}, f32[128,128]{1,0:T(8,128)S(1)}, ...), branch_computations={%region_10.10_spmd, %region_11.11_spmd} | conditional | flops 245776384 | bytes 11370562 | solution.py:197
  470.6 7.1 %conditional.7 = ((f32[1,128,12,128]{1,3,2,0:T(8,128)S(1)}, f32[1,128,12,128]{1,3,2,0:T(8,128)S(1)})) conditional(s32[]{:T(128)} %convert_element_type.155, (f32[1,128,12,128]{1,3,2,0:T(8,128)S(1)}, f32[1,128,12,128]{1,3,2,0:T(8,128)S(1)}) %tuple.155, (s32[]{:T(128)}, bf16[1,2048,1536]{1,2,0:T(8,128)(2,1)}, f32[128,128]{1,0:T(8,128)S(1)}, ...), branch_computations={%region_10.10_spmd, %region_11.11_spmd} | conditional | flops 245776384 | bytes 11370562 | solution.py:197
  479.5 7.1 %conditional.7 = ((f32[1,128,12,128]{1,3,2,0:T(8,128)S(1)}, f32[1,128,12,128]{1,3,2,0:T(8,128)S(1)})) conditional(s32[]{:T(128)} %convert_element_type.155, (f32[1,128,12,128]{1,3,2,0:T(8,128)S(1)}, f32[1,128,12,128]{1,3,2,0:T(8,128)S(1)}) %tuple.155, (s32[]{:T(128)}, bf16[1,2048,1536]{1,2,0:T(8,128)(2,1)}, f32[128,128]{1,0:T(8,128)S(1)}, ...), branch_computations={%region_10.10_spmd, %region_11.11_spmd} | conditional | flops 245776384 | bytes 11370562 | solution.py:197
  488.3 7.1 %conditional.7 = ((f32[1,128,12,128]{1,3,2,0:T(8,128)S(1)}, f32[1,128,12,128]{1,3,2,0:T(8,128)S(1)})) conditional(s32[]{:T(128)} %convert_element_type.155, (f32[1,128,12,128]{1,3,2,0:T(8,128)S(1)}, f32[1,128,12,128]{1,3,2,0:T(8,128)S(1)}) %tuple.155, (s32[]{:T(128)}, bf16[1,2048,1536]{1,2,0:T(8,128)(2,1)}, f32[128,128]{1,0:T(8,128)S(1)}, ...), branch_computations={%region_10.10_spmd, %region_11.11_spmd} | conditional | flops 245776384 | bytes 11370562 | solution.py:197
  500.8 7.1 %conditional.7 = ((f32[1,128,12,128]{1,3,2,0:T(8,128)S(1)}, f32[1,128,12,128]{1,3,2,0:T(8,128)S(1)})) conditional(s32[]{:T(128)} %convert_element_type.155, (f32[1,128,12,128]{1,3,2,0:T(8,128)S(1)}, f32[1,128,12,128]{1,3,2,0:T(8,128)S(1)}) %tuple.155, (s32[]{:T(128)}, bf16[1,2048,1536]{1,2,0:T(8,128)(2,1)}, f32[128,128]{1,0:T(8,128)S(1)}, ...), branch_computations={%region_10.10_spmd, %region_11.11_spmd} | conditional | flops 245776384 | bytes 11370562 | solution.py:197
  (307 shorter events, 147.8 us)
Async XLA Ops:
  7.2 8.1 %copy-start = (f32[16,12,16]{2,0,1:T(8,128)S(1)}, f32[16,12,16]{2,0,1:T(8,128)}, u32[]{:S(2)}) copy-start(f32[16,12,16]{2,0,1:T(8,128)} %param.23) | copy-start | bytes 36868
  7.2 11.6 %copy-start.7 = (u32[256]{0:T(256)S(1)}, u32[256]{0:T(256)}, u32[]{:S(2)}) copy-start(u32[256]{0:T(256)} %constant.273) | copy-start | bytes 3076
  7.2 7.8 %copy-start.3 = (bf16[1,128,1536]{2,1,0:T(8,128)(2,1)S(1)}, bf16[1,128,1536]{2,1,0:T(8,128)(2,1)}, u32[]{:S(2)}) copy-start(bf16[1,128,1536]{2,1,0:T(8,128)(2,1)} %param.20) | copy-start | bytes 1179652
  7.2 8.0 %copy-start.6 = (s32[16]{0:T(128)S(1)}, s32[16]{0:T(128)}, u32[]{:S(2)}) copy-start(s32[16]{0:T(128)} %param.25) | copy-start | bytes 196
  7.2 8.1 %copy-start.4 = (s32[16,16]{1,0:T(8,128)S(1)}, s32[16,16]{1,0:T(8,128)}, u32[]{:S(2)}) copy-start(s32[16,16]{1,0:T(8,128)} %param.24) | copy-start | bytes 3076
  7.2 9.7 %copy-start.5 = (f32[1,128,12]{1,0,2:T(1,128)S(1)}, f32[1,128,12]{1,0,2:T(1,128)}, u32[]{:S(2)}) copy-start(f32[1,128,12]{1,0,2:T(1,128)} %param.22) | copy-start | bytes 18436
  7.2 109.3 %all-gather.5.cloned.1.call-start = ((), (), s32[]{:S(2)}) async-start(), calls=%async_computation | async-start | bytes 6684672 | tf_op jit(solution)/shard_map/all_gather | solution.py:204
  9.3 7.6 %copy-start.1 = (bf16[1,128,1536]{1,2,0:T(8,128)(2,1)S(1)}, bf16[1,128,1536]{1,2,0:T(8,128)(2,1)}, u32[]{:S(2)}) copy-start(bf16[1,128,1536]{1,2,0:T(8,128)(2,1)} %copy.86) | copy-start | bytes 1179652
  9.3 209.8 %all-gather.7.cloned.1.call-start = ((), (), s32[]{:S(2)}) async-start(), calls=%async_computation.1 | async-start | bytes 6684672 | tf_op jit(solution)/shard_map/all_gather | solution.py:205
  11.3 6.5 %copy-start.2 = (bf16[1,128,1536]{1,2,0:T(8,128)(2,1)S(1)}, bf16[1,128,1536]{1,2,0:T(8,128)(2,1)}, u32[]{:S(2)}) copy-start(bf16[1,128,1536]{1,2,0:T(8,128)(2,1)} %copy.90) | copy-start | bytes 1179652
  11.4 379.3 %all-gather.9.cloned.1.call-start = ((), (), s32[]{:S(2)}) async-start(), calls=%async_computation.2 | async-start | bytes 13369344 | tf_op jit(solution)/shard_map/all_gather | solution.py:17
Sparse Core Ops, SparseCore 0:
  11.0 105.4 all-gather.4
  119.5 99.6 all-gather.6
  221.6 169.0 all-gather.8
where the time goes:
time: 519 us; the launch traced here: 516 us
  waiting for transfers between devices  213 us (41%)
  blocking collectives  108 us (21%)
  matrix products  104 us (20%)
  local copies, waits for them, and re-layouts  51.3 us (10%)
  loops' own time  23.2 us (4%)
  between operations  14 us (3%)
    all_gather x1, waiting for transfers between devices, shards(): lax.all_gather(value_rows, 'gene', axis=1, tiled=True)  103 us
    all_gather x1, waiting for transfers between devices, in_one_piece(): lax.all_gather(both, axis, axis=dim, tiled=True)  97.8 us
    dot_general x47, matrix products, pair_slice(): jnp.einsum('hrj,kj->hrk', picked, col_hot, precision=lax.Precision.HIGHEST)  49.1 us
    all_gather x1, blocking collectives, shards(): lax.all_gather(row_lse, 'gene', axis=1, tiled=True)  45 us
    all_gather x1, blocking collectives, shards(): lax.all_gather(row_delta, 'gene', axis=1, tiled=True)  38 us
    unnamed x1, blocking collectives  24.7 us
    another operation x2, loops' own time, over_blocks(): return lax.fori_loop(0, length // BLOCK, step_block, running)  21.9 us
    dot_general x15, matrix products, score_terms(): jnp.einsum('crhd,ckhd->chrk', query_heads, key_heads, preferred_element_t...  21.7 us
  transfers between devices with their start and end apart: 3, of which 3 were waited for; matrix products, arithmetic and copies ran while one was open for 9% of the time, Pallas kernels for 0%

commit v1 on v0

v1 whole, which is shorter than its diff:
```python
import functools
import math

import jax
import jax.numpy as jnp
from jax import lax
from jax.experimental import pallas as pl
from jax.experimental.pallas import tpu as pltpu
from jax.sharding import PartitionSpec as P

MESH = pl.DeviceIdType.MESH
BLOCK = 128
SIDE = 4
CHUNK = 512
LOG2E = 1.4426950408889634
OFF = -1.0e30
BF16 = jnp.bfloat16
F32 = jnp.float32


def nt_dot(a, b):
    return lax.dot_general(a, b, (((1,), (1,)), ((), ())), preferred_element_type=F32)


def nn_dot(a, b):
    return jnp.dot(a, b, preferred_element_type=F32)


def kernel(
    heads,
    genes,
    cells,
    q_in,
    k_in,
    v_in,
    o_in,
    g_in,
    lse_in,
    bias_in,
    index_in,
    count_in,
    dq_out,
    dk_out,
    dv_out,
    bias_out,
    qf,
    kf,
    vf,
    gf,
    statf,
    o_own,
    g_own,
    stat,
    square,
    kt,
    addend,
    weights,
    grads,
    colsum,
    dq,
    dk,
    dv,
    terms,
    mine,
    packed,
    everyones,
    load_sem,
    in_send,
    in_recv,
    out_send,
    out_recv,
    term_send,
    term_recv,
    cell_send,
    cell_recv,
):
    gene = lax.axis_index("gene")
    cell = lax.axis_index("cell")
    row, col = gene // SIDE, gene % SIDE
    turn = 2 * (cell % 2) + (cell // 2) % 2
    live_heads = heads // SIDE
    scale = 1.0 / math.sqrt(BLOCK)

    def slot_of(r, c):
        return (r + c + turn) % SIDE

    place = slot_of(row, col)
    active = place < live_heads
    head = live_heads * col + place
    head_cols = pl.ds(pl.multiple_of(head * BLOCK, BLOCK), BLOCK)

    def peer(step):
        r, c = (row + step // SIDE) % SIDE, (col + step % SIDE) % SIDE
        return r, c, r * SIDE + c

    def block_of(i):
        return pl.ds(pl.multiple_of(i * BLOCK, BLOCK), BLOCK)

    barrier = pltpu.get_barrier_semaphore()
    for step in range(1, genes):
        pl.semaphore_signal(barrier, inc=1, device_id={"gene": peer(step)[2]}, device_id_type=MESH)
    for step in range(1, cells):
        pl.semaphore_signal(
            barrier, inc=1, device_id={"cell": (cell + step) % cells}, device_id_type=MESH
        )

    load_o = pltpu.make_async_copy(o_in.at[0], o_own, load_sem.at[0])
    load_g = pltpu.make_async_copy(g_in.at[0], g_own, load_sem.at[1])
    load_o.start()
    load_g.start()
    stat[...] = jnp.zeros_like(stat)
    square[...] = jnp.zeros_like(square)
    terms[...] = jnp.zeros_like(terms)
    packed[...] = jnp.zeros_like(packed)
    square[:, 0:heads] = lse_in[0]
    lanes = lax.broadcasted_iota(jnp.int32, (BLOCK, BLOCK), 1)
    turned = square[...].T
    for h in range(heads):
        stat[h, 0:1, :] = turned[h : h + 1, :]
    load_o.wait()
    load_g.wait()
    deltas = jnp.zeros((BLOCK, BLOCK), F32)
    for h in range(heads):
        cols = slice(h * BLOCK, (h + 1) * BLOCK)
        one = jnp.sum(
            g_own[:, cols].astype(F32) * o_own[:, cols].astype(F32), axis=1, keepdims=True
        )
        deltas = jnp.where(lanes == h, one, deltas)
    turned = deltas.T
    for h in range(heads):
        stat[h, 1:2, :] = turned[h : h + 1, :]

    pl.semaphore_wait(barrier, genes + cells - 2)

    moved = ((k_in, kf), (q_in, qf), (g_in, gf), (v_in, vf))

    def send_array(a, src, dst):
        for step in range(1, genes):
            r, c, to = peer(step)
            spot = slot_of(r, c)

            @pl.when(spot < live_heads)
            def _():
                cols = pl.ds(pl.multiple_of((live_heads * c + spot) * BLOCK, BLOCK), BLOCK)
                pltpu.make_async_remote_copy(
                    src_ref=src.at[0, :, cols],
                    dst_ref=dst.at[block_of(gene), :],
                    send_sem=in_send.at[a],
                    recv_sem=in_recv.at[a],
                    device_id={"gene": to},
                    device_id_type=MESH,
                ).start()

        @pl.when(active)
        def _():
            pltpu.make_async_copy(
                src.at[0, :, head_cols], dst.at[block_of(gene), :], in_recv.at[a]
            ).start()

    send_array(0, *moved[0])
    send_array(1, *moved[1])
    for step in range(1, genes):
        r, c, to = peer(step)
        spot = slot_of(r, c)

        @pl.when(spot < live_heads)
        def _():
            pltpu.make_async_remote_copy(
                src_ref=stat.at[live_heads * c + spot],
                dst_ref=statf.at[gene],
                send_sem=in_send.at[4],
                recv_sem=in_recv.at[4],
                device_id={"gene": to},
                device_id_type=MESH,
            ).start()

    @pl.when(active)
    def _():
        pltpu.make_async_copy(stat.at[head], statf.at[gene], in_recv.at[4]).start()

    send_array(2, *moved[2])
    send_array(3, *moved[3])

    def arrived(ref, sem):
        pltpu.make_async_copy(ref, ref, sem).wait()

    def give_back(a, src, dst, step):
        _, _, to = peer(step)

        @pl.when(to == gene)
        def _():
            pltpu.make_async_copy(
                src.at[block_of(to), :], dst.at[0, :, head_cols], out_recv.at[a]
            ).start()

        @pl.when(to != gene)
        def _():
            pltpu.make_async_remote_copy(
                src_ref=src.at[block_of(to), :],
                dst_ref=dst.at[0, :, head_cols],
                send_sem=out_send.at[a],
                recv_sem=out_recv.at[a],
                device_id={"gene": to},
                device_id_type=MESH,
            ).start()

    keys_iota = lax.broadcasted_iota(jnp.int32, (genes, genes), 0)
    slot_iota = lax.broadcasted_iota(jnp.int32, (genes, genes), 1)

    def listed(i):
        return (index_in[i : i + 1, :] == keys_iota) & (slot_iota < count_in[i])

    @pl.when(active)
    def _():
        arrived(statf, in_recv.at[4])
        for i in range(genes):
            hit = listed(i)
            bias_row = bias_in[i, pl.ds(head, 1), :]
            bias_col = jnp.sum(jnp.where(hit, bias_row, 0.0), axis=1, keepdims=True)
            hit_col = jnp.sum(jnp.where(hit, 1.0, 0.0), axis=1, keepdims=True)
            start = jnp.where(hit_col > 0.5, bias_col * LOG2E, OFF)
            addend[:, i * BLOCK : (i + 1) * BLOCK] = start - statf[i, 0:1, :] * LOG2E
        arrived(kf, in_recv.at[0])

        def turn_keys(i, carry):
            kt[:, block_of(i)] = kf[block_of(i), :].T
            return carry

        lax.fori_loop(0, genes, turn_keys, 0)
        arrived(qf, in_recv.at[1])
        arrived(gf, in_recv.at[2])

        def value_step(step, carry):
            _, _, j = peer(step)
            own = kf[block_of(j), :]
            total = jnp.zeros((BLOCK, BLOCK), F32)
            for n in range(genes * BLOCK // CHUNK):
                span = slice(n * CHUNK, (n + 1) * CHUNK)
                scores = nt_dot(own, qf[span, :])
                w = jnp.exp2(scores * (scale * LOG2E) + addend[pl.ds(j, 1), span])
                weights[block_of(j), span] = w
                total = total + nn_dot(w.astype(BF16), gf[span, :])
            dv[block_of(j), :] = total.astype(BF16)

            @pl.when(step > 0)
            def _():
                give_back(2, dv, dv_out, step - 1)

            return carry

        lax.fori_loop(0, genes, value_step, 0)
        arrived(vf, in_recv.at[3])
        give_back(2, dv, dv_out, genes - 1)

        def key_step(step, carry):
            _, _, j = peer(step)
            own = vf[block_of(j), :]
            total = jnp.zeros((BLOCK, BLOCK), F32)
            for n in range(genes * BLOCK // CHUNK):
                span = slice(n * CHUNK, (n + 1) * CHUNK)
                wg = nt_dot(own, gf[span, :])
                delta = jnp.concatenate(
                    [statf[n * (CHUNK // BLOCK) + b, 1:2, :] for b in range(CHUNK // BLOCK)], axis=1
                )
                ds = weights[block_of(j), span] * (wg - delta)
                colsum[pl.ds(j, 1), span] = jnp.sum(ds, axis=0, keepdims=True)
                low = ds.astype(BF16)
                grads[block_of(j), span] = low
                total = total + nn_dot(low, qf[span, :])
            dk[block_of(j), :] = (total * scale).astype(BF16)

            @pl.when(step > 0)
            def _():
                give_back(1, dk, dk_out, step - 1)

            return carry

        lax.fori_loop(0, genes, key_step, 0)
        for i in range(genes):
            sums = jnp.sum(colsum[:, i * BLOCK : (i + 1) * BLOCK], axis=1, keepdims=True)
            terms[i, 0:1, 0:genes] = jnp.sum(jnp.where(listed(i), sums, 0.0), axis=0, keepdims=True)
        give_back(1, dk, dk_out, genes - 1)

        def query_step(step, carry):
            _, _, i = peer(step)
            across = nn_dot(kt[...], grads[:, block_of(i)])
            dq[block_of(i), :] = (across.T * scale).astype(BF16)

            @pl.when(step > 0)
            def _():
                give_back(0, dq, dq_out, step - 1)

            @pl.when(step == 0)
            def _():
                for to_step in range(1, genes):
                    to = peer(to_step)[2]
                    pltpu.make_async_remote_copy(
                        src_ref=terms.at[to],
                        dst_ref=mine.at[head],
                        send_sem=term_send,
                        recv_sem=term_recv,
                        device_id={"gene": to},
                        device_id_type=MESH,
                    ).start()
                pltpu.make_async_copy(terms.at[gene], mine.at[head], term_recv).start()

            return carry

        lax.fori_loop(0, genes, query_step, 0)

    arrived(mine, term_recv)
    for h in range(heads):
        packed[h : h + 1, :] = mine[h, 0:1, :]

    @pl.when(active)
    def _():
        give_back(0, dq, dq_out, genes - 1)

    for step in range(1, cells):
        pltpu.make_async_remote_copy(
            src_ref=packed,
            dst_ref=everyones.at[cell],
            send_sem=cell_send,
            recv_sem=cell_recv,
            device_id={"cell": (cell + step) % cells},
            device_id_type=MESH,
        ).start()
    own_packed = pltpu.make_async_copy(packed, everyones.at[cell], cell_recv)
    own_packed.start()
    arrived(everyones, cell_recv)
    everything = jnp.sum(everyones[...], axis=0)
    slot_lanes = lax.broadcasted_iota(jnp.int32, everything.shape, 1)
    picked = jnp.sum(jnp.where(slot_lanes == cell, everything, 0.0), axis=1, keepdims=True)
    bias_out[0] = picked[0:heads, :]

    for a, out in enumerate((dq_out, dk_out, dv_out)):
        arrived(out, out_recv.at[a])

    def sent(ref, count, sem):
        part = ref.at[pl.ds(0, count)]
        pltpu.make_async_copy(part, part, sem).wait()

    @pl.when(active)
    def _():
        for a in range(4):
            sent(kf, (heads - 1) * BLOCK, in_send.at[a])
        sent(statf, heads - 1, in_send.at[4])
        for a in range(3):
            sent(dq, (genes - 1) * BLOCK, out_send.at[a])
        sent(terms, genes - 1, term_send)

    @pl.when(jnp.logical_not(active))
    def _():
        for a in range(4):
            sent(kf, heads * BLOCK, in_send.at[a])
        sent(statf, heads, in_send.at[4])

    if cells > 1:
        sent(everyones, cells - 1, cell_send)


def shards(
    query_rows,
    key_rows,
    value_rows,
    output_rows,
    output_grad,
    row_lse,
    block_bias,
    block_index,
    block_count,
):
    heads = row_lse.shape[2]
    genes = block_index.shape[0]
    cells = lax.axis_size("cell")
    rows = genes * BLOCK
    anywhere = pl.BlockSpec(memory_space=pl.ANY)
    vmem = pl.BlockSpec(memory_space=pltpu.VMEM)
    smem = pl.BlockSpec(memory_space=pltpu.SMEM)
    flat = jax.ShapeDtypeStruct(query_rows.shape, BF16)
    dma = pltpu.SemaphoreType.DMA
    return pl.pallas_call(
        functools.partial(kernel, heads, genes, cells),
        out_shape=(flat, flat, flat, jax.ShapeDtypeStruct((1, heads, 1), F32)),
        in_specs=[anywhere] * 5 + [vmem, vmem, vmem, smem],
        out_specs=(anywhere, anywhere, anywhere, vmem),
        scratch_shapes=[
            pltpu.VMEM((rows, BLOCK), BF16),
            pltpu.VMEM((rows, BLOCK), BF16),
            pltpu.VMEM((rows, BLOCK), BF16),
            pltpu.VMEM((rows, BLOCK), BF16),
            pltpu.VMEM((genes, 8, BLOCK), F32),
            pltpu.VMEM((BLOCK, heads * BLOCK), BF16),
            pltpu.VMEM((BLOCK, heads * BLOCK), BF16),
            pltpu.VMEM((heads, 8, BLOCK), F32),
            pltpu.VMEM((BLOCK, BLOCK), F32),
            pltpu.VMEM((BLOCK, rows), BF16),
            pltpu.VMEM((genes, rows), F32),
            pltpu.VMEM((rows, rows), F32),
            pltpu.VMEM((rows, rows), BF16),
            pltpu.VMEM((genes, rows), F32),
            pltpu.VMEM((rows, BLOCK), BF16),
            pltpu.VMEM((rows, BLOCK), BF16),
            pltpu.VMEM((rows, BLOCK), BF16),
            pltpu.VMEM((genes, 8, BLOCK), F32),
            pltpu.VMEM((heads, 8, BLOCK), F32),
            pltpu.VMEM((16, BLOCK), F32),
            pltpu.VMEM((cells, 16, BLOCK), F32),
            dma((2,)),
            dma((5,)),
            dma((5,)),
            dma((3,)),
            dma((3,)),
            dma,
            dma,
            dma,
            dma,
        ],
        compiler_params=pltpu.CompilerParams(
            collective_id=0, has_side_effects=True, vmem_limit_bytes=48 * 1024 * 1024
        ),
    )(
        query_rows,
        key_rows,
        value_rows,
        output_rows,
        output_grad,
        row_lse,
        block_bias,
        block_index,
        block_count,
    )


def solution(mesh):
    in_specs = (
        P("cell", "gene", None),
        P("cell", "gene", None),
        P("cell", "gene", None),
        P("cell", "gene", None),
        P("cell", "gene", None),
        P("cell", "gene", None),
        P(),
        P(),
        P(),
    )
    out_specs = (
        P("cell", "gene", None),
        P("cell", "gene", None),
        P("cell", "gene", None),
        P("gene", None, "cell"),
    )
    return jax.shard_map(shards, mesh=mesh, in_specs=in_specs, out_specs=out_specs, check_vma=False)
```

time: 519 us -> 96.3 us (0.19)
  the two profiles are of different devices: /device:TPU:131 before, /device:TPU:2 now
where the time goes in v1:
time: 96.3 us; the launch traced here: 95.1 us
  Pallas kernels  84.9 us (88%)
  local copies, waits for them, and re-layouts  9.55 us (10%)
    pallas_call x1, Pallas kernels, shards(): pl.pallas_call(functools.partial(kernel, heads, genes, cells), out_shape=...  84.9 us
    unnamed x19, local copies, waits for them, and re-layouts  8.95 us

profile of v1, /device:TPU:2, one launch (start us, length us, event | category | flops | bytes accessed | tf_op | source)
XLA Modules:
  0.0 95.1 jit_solution(1477415506743367520)
XLA Ops:
  0.6 0.8 copy.13.lse_in
  1.4 0.0 copy-start.5
  1.4 0.0 copy-start.6
  1.4 0.9 copy.14.bias_in
  2.4 0.0 copy-done.5
  2.4 0.0 copy-done.6
  2.4 0.0 copy-start
  2.4 1.0 %copy-done = bf16[1,128,1536]{2,1,0:T(8,128)(2,1)S(1)} copy-done((bf16[1,128,1536]{2,1,0:T(8,128)(2,1)S(1)}, bf16[1,128,1536]{2,1,0:T(8,128)(2,1)}, u32[]{:S(2)}) %copy-start) | copy-done | bytes 393240
  3.4 0.0 copy-start.1
  3.4 1.0 %copy-done.1 = bf16[1,128,1536]{2,1,0:T(8,128)(2,1)S(1)} copy-done((bf16[1,128,1536]{2,1,0:T(8,128)(2,1)S(1)}, bf16[1,128,1536]{2,1,0:T(8,128)(2,1)}, u32[]{:S(2)}) %copy-start.1) | copy-done | bytes 393240
  4.4 0.0 copy-start.2
  4.4 1.0 %copy-done.2 = bf16[1,128,1536]{2,1,0:T(8,128)(2,1)S(1)} copy-done((bf16[1,128,1536]{2,1,0:T(8,128)(2,1)S(1)}, bf16[1,128,1536]{2,1,0:T(8,128)(2,1)}, u32[]{:S(2)}) %copy-start.2) | copy-done | bytes 393240
  5.4 0.0 copy-start.3
  5.4 1.0 %copy-done.3 = bf16[1,128,1536]{2,1,0:T(8,128)(2,1)S(1)} copy-done((bf16[1,128,1536]{2,1,0:T(8,128)(2,1)S(1)}, bf16[1,128,1536]{2,1,0:T(8,128)(2,1)}, u32[]{:S(2)}) %copy-start.3) | copy-done | bytes 393240
  6.4 0.0 copy-start.4
  6.4 1.0 %copy-done.4 = bf16[1,128,1536]{2,1,0:T(8,128)(2,1)S(1)} copy-done((bf16[1,128,1536]{2,1,0:T(8,128)(2,1)S(1)}, bf16[1,128,1536]{2,1,0:T(8,128)(2,1)}, u32[]{:S(2)}) %copy-start.4) | copy-done | bytes 393240
  7.4 84.9 %shard_map.120 = (bf16[1,128,1536]{2,1,0:T(8,128)(2,1)S(1)}, bf16[1,128,1536]{2,1,0:T(8,128)(2,1)S(1)}, bf16[1,128,1536]{2,1,0:T(8,128)(2,1)S(1)}, f32[1,12,1]{2,1,0:T(8,128)S(1)}) custom-call(bf16[1,128,1536]{2,1,0:T(8,128)(2,1)S(1)} %copy-done, bf16[1,128,1536]{2,1,0:T(8,128)(2,1)S(1)} %copy-done.1, bf16[1,128,1536]{2,1,0:T(8,128)(2,1)S(1)} %copy-done.2, ...), custom_call_target="tpu_custom_call" | custom-call | tf_op jit(solution)/shard_map/pallas_call | solution.py:382
  92.3 0.6 copy.15
  92.9 0.7 copy.19
  93.6 0.7 copy.20
  94.4 0.7 copy.21
Async XLA Ops:
  1.4 1.0 %copy-start.5 = (s32[16,16]{1,0:T(8,128)S(1)}, s32[16,16]{1,0:T(8,128)}, u32[]{:S(2)}) copy-start(s32[16,16]{1,0:T(8,128)} %index_in.1) | copy-start | bytes 3076
  1.4 1.0 %copy-start.6 = (s32[16]{0:T(128)S(1)}, s32[16]{0:T(128)}, u32[]{:S(2)}) copy-start(s32[16]{0:T(128)} %count_in.1) | copy-start | bytes 196
  2.4 1.0 %copy-start = (bf16[1,128,1536]{2,1,0:T(8,128)(2,1)S(1)}, bf16[1,128,1536]{2,1,0:T(8,128)(2,1)}, u32[]{:S(2)}) copy-start(bf16[1,128,1536]{2,1,0:T(8,128)(2,1)} %q_in.1) | copy-start | bytes 1179652
  3.4 1.0 %copy-start.1 = (bf16[1,128,1536]{2,1,0:T(8,128)(2,1)S(1)}, bf16[1,128,1536]{2,1,0:T(8,128)(2,1)}, u32[]{:S(2)}) copy-start(bf16[1,128,1536]{2,1,0:T(8,128)(2,1)} %k_in.1) | copy-start | bytes 1179652
  4.4 1.0 %copy-start.2 = (bf16[1,128,1536]{2,1,0:T(8,128)(2,1)S(1)}, bf16[1,128,1536]{2,1,0:T(8,128)(2,1)}, u32[]{:S(2)}) copy-start(bf16[1,128,1536]{2,1,0:T(8,128)(2,1)} %v_in.1) | copy-start | bytes 1179652
  5.4 1.0 %copy-start.3 = (bf16[1,128,1536]{2,1,0:T(8,128)(2,1)S(1)}, bf16[1,128,1536]{2,1,0:T(8,128)(2,1)}, u32[]{:S(2)}) copy-start(bf16[1,128,1536]{2,1,0:T(8,128)(2,1)} %o_in.1) | copy-start | bytes 1179652
  6.4 1.0 %copy-start.4 = (bf16[1,128,1536]{2,1,0:T(8,128)(2,1)S(1)}, bf16[1,128,1536]{2,1,0:T(8,128)(2,1)}, u32[]{:S(2)}) copy-start(bf16[1,128,1536]{2,1,0:T(8,128)(2,1)} %g_in.1) | copy-start | bytes 1179652

commit v2 on v1

v2 whole, which is shorter than its diff:
```python
import functools
import math

import jax
import jax.numpy as jnp
from jax import lax
from jax.experimental import pallas as pl
from jax.experimental.pallas import tpu as pltpu
from jax.sharding import PartitionSpec as P

MESH = pl.DeviceIdType.MESH
BLOCK = 128
SIDE = 4
WIDE = 256
TALL = 512
LOG2E = 1.4426950408889634
OFF = -1.0e30
BF16 = jnp.bfloat16
F32 = jnp.float32


def nt_dot(a, b):
    return lax.dot_general(a, b, (((1,), (1,)), ((), ())), preferred_element_type=F32)


def nn_dot(a, b):
    return jnp.dot(a, b, preferred_element_type=F32)


def kernel(
    heads,
    genes,
    cells,
    q_in,
    k_in,
    v_in,
    o_in,
    g_in,
    lse_in,
    bias_in,
    index_in,
    count_in,
    dq_out,
    dk_out,
    dv_out,
    bias_out,
    qf,
    kf,
    vf,
    gf,
    statf,
    o_own,
    g_own,
    stat,
    square,
    kt,
    addend,
    weights,
    low,
    colsum,
    dq,
    dk,
    dv,
    terms,
    mine,
    everyones,
    lse_own,
    bias_own,
    index_own,
    count_own,
    load_sem,
    in_send,
    in_recv,
    out_send,
    out_recv,
    term_send,
    term_recv,
    cell_send,
    cell_recv,
):
    gene = lax.axis_index("gene")
    cell = lax.axis_index("cell")
    row, col = gene // SIDE, gene % SIDE
    turn = 2 * (cell % 2) + (cell // 2) % 2
    live_heads = heads // SIDE
    scale = 1.0 / math.sqrt(BLOCK)

    def slot_of(r, c):
        return (r + turn) % SIDE

    place = slot_of(row, col)
    active = place < live_heads
    head = live_heads * col + place
    head_cols = pl.ds(pl.multiple_of(head * BLOCK, BLOCK), BLOCK)

    def peer(step):
        r, c = (row + step // SIDE) % SIDE, (col + step % SIDE) % SIDE
        return r, c, r * SIDE + c

    def block_of(i):
        return pl.ds(pl.multiple_of(i * BLOCK, BLOCK), BLOCK)

    barrier = pltpu.get_barrier_semaphore()
    for step in range(1, genes):
        pl.semaphore_signal(barrier, inc=1, device_id={"gene": peer(step)[2]}, device_id_type=MESH)
    for step in range(1, cells):
        pl.semaphore_signal(
            barrier, inc=1, device_id={"cell": (cell + step) % cells}, device_id_type=MESH
        )

    loads = [
        pltpu.make_async_copy(src, dst, load_sem.at[n])
        for n, (src, dst) in enumerate(
            (
                (o_in.at[0], o_own),
                (g_in.at[0], g_own),
                (lse_in, lse_own),
                (bias_in, bias_own),
                (index_in, index_own),
                (count_in, count_own),
            )
        )
    ]
    for load in loads:
        load.start()
    pl.semaphore_wait(barrier, genes + cells - 2)

    moved = ((k_in, kf), (q_in, qf), (g_in, gf), (v_in, vf))

    def send_array(a, src, dst):
        for step in range(1, genes):
            r, c, to = peer(step)
            spot = slot_of(r, c)

            @pl.when(spot < live_heads)
            def _():
                cols = pl.ds(pl.multiple_of((live_heads * c + spot) * BLOCK, BLOCK), BLOCK)
                pltpu.make_async_remote_copy(
                    src_ref=src.at[0, :, cols],
                    dst_ref=dst.at[block_of(gene), :],
                    send_sem=in_send.at[a],
                    recv_sem=in_recv.at[a],
                    device_id={"gene": to},
                    device_id_type=MESH,
                ).start()

        @pl.when(active)
        def _():
            pltpu.make_async_copy(
                src.at[0, :, head_cols], dst.at[block_of(gene), :], in_recv.at[a]
            ).start()

    send_array(0, *moved[0])
    send_array(1, *moved[1])
    terms[...] = jnp.zeros_like(terms)
    lanes = lax.broadcasted_iota(jnp.int32, (BLOCK, BLOCK), 1)
    for load in loads:
        load.wait()
    deltas = jnp.zeros((BLOCK, BLOCK), F32)
    for h in range(heads):
        cols = slice(h * BLOCK, (h + 1) * BLOCK)
        one = jnp.sum(
            g_own[:, cols].astype(F32) * o_own[:, cols].astype(F32), axis=1, keepdims=True
        )
        deltas = jnp.where(lanes == h, one, deltas)
    turned = deltas.T
    for h in range(heads):
        stat[h, 0:1, :] = lse_own[h]
        stat[h, 1:2, :] = turned[h : h + 1, :]

    for step in range(1, genes):
        r, c, to = peer(step)
        spot = slot_of(r, c)

        @pl.when(spot < live_heads)
        def _():
            pltpu.make_async_remote_copy(
                src_ref=stat.at[live_heads * c + spot],
                dst_ref=statf.at[gene],
                send_sem=in_send.at[4],
                recv_sem=in_recv.at[4],
                device_id={"gene": to},
                device_id_type=MESH,
            ).start()

    @pl.when(active)
    def _():
        pltpu.make_async_copy(stat.at[head], statf.at[gene], in_recv.at[4]).start()

    send_array(2, *moved[2])
    send_array(3, *moved[3])

    def arrived(ref, sem):
        pltpu.make_async_copy(ref, ref, sem).wait()

    def give_back(a, src, dst, to):
        @pl.when(to == gene)
        def _():
            pltpu.make_async_copy(
                src.at[block_of(to), :], dst.at[0, :, head_cols], out_recv.at[a]
            ).start()

        @pl.when(to != gene)
        def _():
            pltpu.make_async_remote_copy(
                src_ref=src.at[block_of(to), :],
                dst_ref=dst.at[0, :, head_cols],
                send_sem=out_send.at[a],
                recv_sem=out_recv.at[a],
                device_id={"gene": to},
                device_id_type=MESH,
            ).start()

    wides = genes * BLOCK // WIDE
    per_wide = WIDE // BLOCK

    def wide_at(step):
        return (gene // per_wide + step) % wides

    def wide_of(n):
        return pl.ds(pl.multiple_of(n * WIDE, WIDE), WIDE)

    def give_wide_back(a, src, dst, step):
        for b in range(per_wide):
            give_back(a, src, dst, wide_at(step) * per_wide + b)

    def over_queries(m, right):
        total = jnp.zeros((WIDE, BLOCK), F32)
        for n in range(wides):
            total = total + nn_dot(low[n, wide_of(m), :], right[n * WIDE : (n + 1) * WIDE, :])
        return total

    keys_iota = lax.broadcasted_iota(jnp.int32, (genes, genes), 0)
    slot_iota = lax.broadcasted_iota(jnp.int32, (genes, genes), 1)

    def listed(i):
        return (index_own[i : i + 1, :] == keys_iota) & (slot_iota < count_own[i])

    @pl.when(active)
    def _():
        arrived(statf, in_recv.at[4])
        for i in range(genes):
            hit = listed(i)
            bias_row = bias_own[head, i : i + 1, :]
            bias_col = jnp.sum(jnp.where(hit, bias_row, 0.0), axis=1, keepdims=True)
            hit_col = jnp.sum(jnp.where(hit, 1.0, 0.0), axis=1, keepdims=True)
            start = jnp.where(hit_col > 0.5, bias_col * LOG2E, OFF)
            n, at = i // per_wide, i % per_wide * BLOCK
            addend[n, :, at : at + BLOCK] = start - statf[i, 0:1, :] * LOG2E
        arrived(kf, in_recv.at[0])

        def turn_keys(i, carry):
            kt[:, block_of(i)] = kf[block_of(i), :].T
            return carry

        lax.fori_loop(0, genes, turn_keys, 0)
        arrived(qf, in_recv.at[1])

        def score_step(n, carry):
            own = qf[wide_of(n), :]
            for m in range(0, genes * BLOCK, TALL):
                scores = nt_dot(kf[m : m + TALL, :], own)
                for b in range(0, TALL, BLOCK):
                    j = (m + b) // BLOCK
                    span = slice(m + b, m + b + BLOCK)
                    w = jnp.exp2(
                        scores[b : b + BLOCK, :] * (scale * LOG2E) + addend[n, j : j + 1, :]
                    )
                    weights[n, span, :] = w
                    low[n, span, :] = w.astype(BF16)
            return carry

        lax.fori_loop(0, wides, score_step, 0)
        arrived(gf, in_recv.at[2])

        def value_step(step, carry):
            m = wide_at(step)
            dv[wide_of(m), :] = over_queries(m, gf).astype(BF16)

            @pl.when(step > 0)
            def _():
                give_wide_back(2, dv, dv_out, step - 1)

            return carry

        lax.fori_loop(0, wides, value_step, 0)
        arrived(vf, in_recv.at[3])
        give_wide_back(2, dv, dv_out, wides - 1)

        def grad_step(step, carry):
            n = wide_at(step)
            own = gf[wide_of(n), :]
            delta = jnp.concatenate(
                [statf[n * per_wide + b, 1:2, :] for b in range(per_wide)], axis=1
            )
            for m in range(0, genes * BLOCK, TALL):
                wg = nt_dot(vf[m : m + TALL, :], own)
                for b in range(0, TALL, BLOCK):
                    j = (m + b) // BLOCK
                    span = slice(m + b, m + b + BLOCK)
                    ds = weights[n, span, :] * (wg[b : b + BLOCK, :] - delta)
                    colsum[n, j : j + 1, :] = jnp.sum(ds, axis=0, keepdims=True)
                    low[n, span, :] = ds.astype(BF16)
            return carry

        lax.fori_loop(0, wides, grad_step, 0)
        for i in range(genes):
            n, at = i // per_wide, i % per_wide * BLOCK
            sums = jnp.sum(colsum[n, :, at : at + BLOCK], axis=1, keepdims=True)
            terms[i, :, 0:genes] = jnp.sum(jnp.where(listed(i), sums, 0.0), axis=0, keepdims=True)

        def query_step(step, carry):
            n = wide_at(step)
            across = nn_dot(kt[...], low[n])
            dq[wide_of(n), :] = (across.T * scale).astype(BF16)

            @pl.when(step > 0)
            def _():
                give_wide_back(0, dq, dq_out, step - 1)

            @pl.when(step == 0)
            def _():
                for to_step in range(1, genes):
                    to = peer(to_step)[2]
                    pltpu.make_async_remote_copy(
                        src_ref=terms.at[to],
                        dst_ref=mine.at[head],
                        send_sem=term_send,
                        recv_sem=term_recv,
                        device_id={"gene": to},
                        device_id_type=MESH,
                    ).start()
                pltpu.make_async_copy(terms.at[gene], mine.at[head], term_recv).start()

            return carry

        lax.fori_loop(0, wides, query_step, 0)
        give_wide_back(0, dq, dq_out, wides - 1)

        def key_step(step, carry):
            m = wide_at(step)
            dk[wide_of(m), :] = (over_queries(m, qf) * scale).astype(BF16)

            @pl.when(step > 0)
            def _():
                give_wide_back(1, dk, dk_out, step - 1)

            return carry

        lax.fori_loop(0, wides, key_step, 0)
        give_wide_back(1, dk, dk_out, wides - 1)

    square[...] = jnp.zeros_like(square)
    arrived(mine, term_recv)
    for step in range(1, cells):
        pltpu.make_async_remote_copy(
            src_ref=mine,
            dst_ref=everyones.at[cell],
            send_sem=cell_send,
            recv_sem=cell_recv,
            device_id={"cell": (cell + step) % cells},
            device_id_type=MESH,
        ).start()
    pltpu.make_async_copy(mine, everyones.at[cell], cell_recv).start()
    arrived(everyones, cell_recv)
    everything = jnp.sum(everyones[...], axis=0)
    for h in range(heads):
        square[h : h + 1, :] = everything[h]
    slot_rows = lax.broadcasted_iota(jnp.int32, (BLOCK, BLOCK), 0)
    picked = jnp.sum(jnp.where(slot_rows == cell, square[...].T, 0.0), axis=0, keepdims=True)
    bias_out[0] = picked[:, 0:heads]

    for a, out in enumerate((dq_out, dk_out, dv_out)):
        arrived(out, out_recv.at[a])

    def sent(ref, count, sem):
        part = ref.at[pl.ds(0, count)]
        pltpu.make_async_copy(part, part, sem).wait()

    @pl.when(active)
    def _():
        for a in range(4):
            sent(kf, (heads - 1) * BLOCK, in_send.at[a])
        sent(statf, heads - 1, in_send.at[4])
        for a in range(3):
            sent(dq, (genes - 1) * BLOCK, out_send.at[a])
        sent(terms, genes - 1, term_send)

    @pl.when(jnp.logical_not(active))
    def _():
        for a in range(4):
            sent(kf, heads * BLOCK, in_send.at[a])
        sent(statf, heads, in_send.at[4])

    if cells > 1:
        sent(everyones, cells - 1, cell_send)


def put_out(*refs):
    count = (len(refs) - 1) // 2
    copies = [
        pltpu.make_async_copy(refs[n], refs[count + n], refs[-1].at[n]) for n in range(count)
    ]
    for copy in copies:
        copy.start()
    for copy in copies:
        copy.wait()


def shards(
    query_rows,
    key_rows,
    value_rows,
    output_rows,
    output_grad,
    row_lse,
    block_bias,
    block_index,
    block_count,
):
    heads = row_lse.shape[2]
    genes = block_index.shape[0]
    cells = lax.axis_size("cell")
    rows = genes * BLOCK
    anywhere = pl.BlockSpec(memory_space=pl.ANY)
    vmem = pl.BlockSpec(memory_space=pltpu.VMEM)
    flat = jax.ShapeDtypeStruct(query_rows.shape, BF16)
    dma = pltpu.SemaphoreType.DMA
    wides = rows // WIDE
    held = pltpu.VMEM(query_rows.shape, BF16)
    bias_flat = (1, 1, heads)
    results = pl.pallas_call(
        functools.partial(kernel, heads, genes, cells),
        out_shape=(held, held, held, pltpu.VMEM(bias_flat, F32)),
        in_specs=[pl.BlockSpec(memory_space=pltpu.HBM)] * 9,
        out_specs=(vmem, vmem, vmem, vmem),
        scratch_shapes=[
            pltpu.VMEM((rows, BLOCK), BF16),
            pltpu.VMEM((rows, BLOCK), BF16),
            pltpu.VMEM((rows, BLOCK), BF16),
            pltpu.VMEM((rows, BLOCK), BF16),
            pltpu.VMEM((genes, 2, BLOCK), F32),
            pltpu.VMEM((BLOCK, heads * BLOCK), BF16),
            pltpu.VMEM((BLOCK, heads * BLOCK), BF16),
            pltpu.VMEM((heads, 2, BLOCK), F32),
            pltpu.VMEM((BLOCK, BLOCK), F32),
            pltpu.VMEM((BLOCK, rows), BF16),
            pltpu.VMEM((wides, genes, WIDE), F32),
            pltpu.VMEM((wides, rows, WIDE), F32),
            pltpu.VMEM((wides, rows, WIDE), BF16),
            pltpu.VMEM((wides, genes, WIDE), F32),
            pltpu.VMEM((rows, BLOCK), BF16),
            pltpu.VMEM((rows, BLOCK), BF16),
            pltpu.VMEM((rows, BLOCK), BF16),
            pltpu.VMEM((genes, 1, BLOCK), F32),
            pltpu.VMEM((heads, 1, BLOCK), F32),
            pltpu.VMEM((cells, heads, 1, BLOCK), F32),
            pltpu.VMEM((heads, 1, BLOCK), F32),
            pltpu.VMEM((heads, genes, genes), F32),
            pltpu.VMEM((genes, genes), jnp.int32),
            pltpu.SMEM((genes,), jnp.int32),
            dma((6,)),
            dma((5,)),
            dma((5,)),
            dma((3,)),
            dma((3,)),
            dma,
            dma,
            dma,
            dma,
        ],
        compiler_params=pltpu.CompilerParams(
            collective_id=0, has_side_effects=True, vmem_limit_bytes=60 * 1024 * 1024
        ),
    )(
        query_rows,
        key_rows,
        value_rows,
        output_rows,
        output_grad,
        jnp.transpose(row_lse, (2, 0, 1)),
        jnp.transpose(block_bias, (1, 0, 2)),
        block_index,
        block_count,
    )
    query_grad, key_grad, value_grad, bias_grad = pl.pallas_call(
        put_out,
        out_shape=(flat, flat, flat, jax.ShapeDtypeStruct(bias_flat, F32)),
        in_specs=[anywhere] * 4,
        out_specs=(anywhere,) * 4,
        scratch_shapes=[dma((4,))],
        compiler_params=pltpu.CompilerParams(vmem_limit_bytes=1024 * 1024),
    )(*(pltpu.with_memory_space_constraint(r, pltpu.VMEM) for r in results))
    return (query_grad, key_grad, value_grad, jnp.transpose(bias_grad, (0, 2, 1)))


def solution(mesh):
    in_specs = (
        P("cell", "gene", None),
        P("cell", "gene", None),
        P("cell", "gene", None),
        P("cell", "gene", None),
        P("cell", "gene", None),
        P("cell", "gene", None),
        P(),
        P(),
        P(),
    )
    out_specs = (
        P("cell", "gene", None),
        P("cell", "gene", None),
        P("cell", "gene", None),
        P("gene", None, "cell"),
    )
    return jax.shard_map(shards, mesh=mesh, in_specs=in_specs, out_specs=out_specs, check_vma=False)
```

time: 96.3 us -> 80.1 us (0.83)
  local copies, waits for them, and re-layouts: 9.55 us -> 0 us
  Pallas kernels: 84.9 us -> 78.8 us
    unnamed x19 -> x0, local copies, waits for them, and re-layouts: 8.95 us -> none
    pallas_call x1, Pallas kernels: 84.9 us -> 77.7 us  [shards(): pl.pallas_call(functools.partial(kernel, heads, genes, cells), out_shape=...]
    pallas_call x0 -> x1, Pallas kernels: none -> 1.04 us  [shards(): pl.pallas_call(put_out, out_shape=(flat, flat, flat, jax.ShapeDtypeStruct...]
where the time goes in v2:
time: 80.1 us; the launch traced here: 79.4 us
  Pallas kernels  78.8 us (98%)
    pallas_call x1, Pallas kernels, shards(): pl.pallas_call(functools.partial(kernel, heads, genes, cells), out_shape=...  77.7 us

profile of v2, /device:TPU:2, one launch (start us, length us, event | category | flops | bytes accessed | tf_op | source)
XLA Modules:
  0.0 79.4 jit_solution(3946891746375674)
XLA Ops:
  0.6 77.7 %shard_map.120 = (bf16[1,128,1536]{2,1,0:T(8,128)(2,1)S(1)}, bf16[1,128,1536]{2,1,0:T(8,128)(2,1)S(1)}, bf16[1,128,1536]{2,1,0:T(8,128)(2,1)S(1)}, f32[1,1,12]{2,1,0:T(1,128)S(1)}) custom-call(bf16[1,128,1536]{2,1,0:T(8,128)(2,1)} %q_in.1, bf16[1,128,1536]{2,1,0:T(8,128)(2,1)} %k_in.1, bf16[1,128,1536]{2,1,0:T(8,128)(2,1)} %v_in.1, ...), custom_call_target="tpu_custom_call" | custom-call | tf_op jit(solution)/shard_map/pallas_call | solution.py:432
  78.4 1.0 %shard_map.121 = (bf16[1,128,1536]{2,1,0:T(8,128)(2,1)}, bf16[1,128,1536]{2,1,0:T(8,128)(2,1)}, bf16[1,128,1536]{2,1,0:T(8,128)(2,1)}, f32[1,1,12]{2,1,0:T(1,128)}) custom-call(bf16[1,128,1536]{2,1,0:T(8,128)(2,1)S(1)} %get-tuple-element.12.refs_0_, bf16[1,128,1536]{2,1,0:T(8,128)(2,1)S(1)} %get-tuple-element.13.refs_1_, ...), custom_call_target="tpu_custom_call" | custom-call | tf_op jit(solution)/shard_map/pallas_call | solution.py:486

commit v3 on v2

--- a/solution.py
+++ b/solution.py
@@ -13,6 +13,7 @@
 SIDE = 4
 WIDE = 256
 TALL = 512
+UNROLL = 4
 LOG2E = 1.4426950408889634
 OFF = -1.0e30
 BF16 = jnp.bfloat16
@@ -64,6 +65,7 @@
     terms,
     mine,
     everyones,
+    relay,
     lse_own,
     bias_own,
     index_own,
@@ -71,8 +73,10 @@
     load_sem,
     in_send,
     in_recv,
+    v_recv,
     out_send,
     out_recv,
+    relay_recv,
     term_send,
     term_recv,
     cell_send,
@@ -81,18 +85,32 @@
     gene = lax.axis_index("gene")
     cell = lax.axis_index("cell")
     row, col = gene // SIDE, gene % SIDE
-    turn = 2 * (cell % 2) + (cell // 2) % 2
+    core, half = cell % 2, (cell // 2) % 2
+    other = cell + 2 - 4 * half
     live_heads = heads // SIDE
     scale = 1.0 / math.sqrt(BLOCK)
 
-    def slot_of(r, c):
-        return (r + turn) % SIDE
-
-    place = slot_of(row, col)
+    def slot_of(r, side):
+        return (r + 2 * core + side) % SIDE
+
+    def device_at(to):
+        return {"cell": other, "gene": to}
+
+    place = slot_of(row, half)
     active = place < live_heads
     head = live_heads * col + place
     head_cols = pl.ds(pl.multiple_of(head * BLOCK, BLOCK), BLOCK)
 
+    beside_row = row + 1 - 2 * (row % 2)
+    beside = beside_row * SIDE + col
+    beside_place = slot_of(beside_row, half)
+    helped = jnp.logical_and(active, beside_place >= live_heads)
+    beside_cols = pl.ds(
+        pl.multiple_of((live_heads * col + beside_place) * BLOCK, BLOCK), BLOCK
+    )
+    way = 2 * half - 1
+    near = 2 * SIDE
+
     def peer(step):
         r, c = (row + step // SIDE) % SIDE, (col + step % SIDE) % SIDE
         return r, c, r * SIDE + c
@@ -101,8 +119,9 @@
         return pl.ds(pl.multiple_of(i * BLOCK, BLOCK), BLOCK)
 
     barrier = pltpu.get_barrier_semaphore()
-    for step in range(1, genes):
-        pl.semaphore_signal(barrier, inc=1, device_id={"gene": peer(step)[2]}, device_id_type=MESH)
+    for step in range(genes):
+        pl.semaphore_signal(barrier, inc=1, device_id=device_at(peer(step)[2]), device_id_type=MESH)
+    pl.semaphore_signal(barrier, inc=1, device_id={"gene": beside}, device_id_type=MESH)
     for step in range(1, cells):
         pl.semaphore_signal(
             barrier, inc=1, device_id={"cell": (cell + step) % cells}, device_id_type=MESH
@@ -123,14 +142,14 @@
     ]
     for load in loads:
         load.start()
-    pl.semaphore_wait(barrier, genes + cells - 2)
+    pl.semaphore_wait(barrier, genes + cells)
 
     moved = ((k_in, kf), (q_in, qf), (g_in, gf), (v_in, vf))
 
-    def send_array(a, src, dst):
-        for step in range(1, genes):
+    def send_array(a, src, dst, recv_sem):
+        for step in range(genes):
             r, c, to = peer(step)
-            spot = slot_of(r, c)
+            spot = slot_of(r, 1 - half)
 
             @pl.when(spot < live_heads)
             def _():
@@ -139,19 +158,13 @@
                     src_ref=src.at[0, :, cols],
                     dst_ref=dst.at[block_of(gene), :],
                     send_sem=in_send.at[a],
-                    recv_sem=in_recv.at[a],
-                    device_id={"gene": to},
+                    recv_sem=recv_sem,
+                    device_id=device_at(to),
                     device_id_type=MESH,
                 ).start()
 
-        @pl.when(active)
-        def _():
-            pltpu.make_async_copy(
-                src.at[0, :, head_cols], dst.at[block_of(gene), :], in_recv.at[a]
-            ).start()
-
-    send_array(0, *moved[0])
-    send_array(1, *moved[1])
+    send_array(0, *moved[0], in_recv.at[0])
+    send_array(1, *moved[1], in_recv.at[1])
     terms[...] = jnp.zeros_like(terms)
     lanes = lax.broadcasted_iota(jnp.int32, (BLOCK, BLOCK), 1)
     for load in loads:
@@ -168,9 +181,9 @@
         stat[h, 0:1, :] = lse_own[h]
         stat[h, 1:2, :] = turned[h : h + 1, :]
 
-    for step in range(1, genes):
+    for step in range(genes):
         r, c, to = peer(step)
-        spot = slot_of(r, c)
+        spot = slot_of(r, 1 - half)
 
         @pl.when(spot < live_heads)
         def _():
@@ -179,35 +192,62 @@
                 dst_ref=statf.at[gene],
                 send_sem=in_send.at[4],
                 recv_sem=in_recv.at[4],
-                device_id={"gene": to},
+                device_id=device_at(to),
                 device_id_type=MESH,
             ).start()
 
-    @pl.when(active)
-    def _():
-        pltpu.make_async_copy(stat.at[head], statf.at[gene], in_recv.at[4]).start()
-
-    send_array(2, *moved[2])
-    send_array(3, *moved[3])
+    send_array(2, *moved[2], in_recv.at[2])
+    send_array(3, *moved[3], v_recv.at[row])
 
     def arrived(ref, sem):
         pltpu.make_async_copy(ref, ref, sem).wait()
 
+    def give_direct(a, src, dst, to):
+        pltpu.make_async_remote_copy(
+            src_ref=src.at[block_of(to), :],
+            dst_ref=dst.at[0, :, head_cols],
+            send_sem=out_send.at[a],
+            recv_sem=out_recv.at[a],
+            device_id=device_at(to),
+            device_id_type=MESH,
+        ).start()
+
+    def place_near(to):
+        return ((to % SIDE - col) * way + 2 * SIDE) % SIDE * SIDE + to // SIDE
+
+    def give_relay(a, src, to):
+        pltpu.make_async_remote_copy(
+            src_ref=src.at[block_of(to), :],
+            dst_ref=relay.at[a, block_of(place_near(to)), :],
+            send_sem=out_send.at[a],
+            recv_sem=relay_recv.at[a],
+            device_id={"gene": beside},
+            device_id_type=MESH,
+        ).start()
+
+    def near_gene(k):
+        return k % SIDE * SIDE + (col + k // SIDE * way + SIDE) % SIDE
+
     def give_back(a, src, dst, to):
-        @pl.when(to == gene)
+        by_relay = jnp.logical_and(helped, place_near(to) < near)
+
+        @pl.when(by_relay)
         def _():
-            pltpu.make_async_copy(
-                src.at[block_of(to), :], dst.at[0, :, head_cols], out_recv.at[a]
-            ).start()
-
-        @pl.when(to != gene)
+            give_relay(a, src, to)
+
+        @pl.when(jnp.logical_not(by_relay))
         def _():
+            give_direct(a, src, dst, to)
+
+    def pass_on(a, dst):
+        arrived(relay.at[a], relay_recv.at[a])
+        for k in range(near):
             pltpu.make_async_remote_copy(
-                src_ref=src.at[block_of(to), :],
-                dst_ref=dst.at[0, :, head_cols],
+                src_ref=relay.at[a, block_of(k), :],
+                dst_ref=dst.at[0, :, beside_cols],
                 send_sem=out_send.at[a],
                 recv_sem=out_recv.at[a],
-                device_id={"gene": to},
+                device_id=device_at(near_gene(k)),
                 device_id_type=MESH,
             ).start()
 
@@ -284,26 +324,31 @@
             return carry
 
         lax.fori_loop(0, wides, value_step, 0)
-        arrived(vf, in_recv.at[3])
         give_wide_back(2, dv, dv_out, wides - 1)
 
-        def grad_step(step, carry):
-            n = wide_at(step)
-            own = gf[wide_of(n), :]
-            delta = jnp.concatenate(
-                [statf[n * per_wide + b, 1:2, :] for b in range(per_wide)], axis=1
-            )
-            for m in range(0, genes * BLOCK, TALL):
-                wg = nt_dot(vf[m : m + TALL, :], own)
-                for b in range(0, TALL, BLOCK):
-                    j = (m + b) // BLOCK
-                    span = slice(m + b, m + b + BLOCK)
-                    ds = weights[n, span, :] * (wg[b : b + BLOCK, :] - delta)
-                    colsum[n, j : j + 1, :] = jnp.sum(ds, axis=0, keepdims=True)
-                    low[n, span, :] = ds.astype(BF16)
-            return carry
-
-        lax.fori_loop(0, wides, grad_step, 0)
+        def part_step(k, carry):
+            part = (row + SIDE - k) % SIDE
+            keys = pl.ds(pl.multiple_of(part * TALL, TALL), TALL)
+            arrived(vf.at[keys, :], v_recv.at[part])
+
+            def grad_step(lap, inner):
+                for n in [lap * UNROLL + u for u in range(UNROLL)]:
+                    delta = jnp.concatenate(
+                        [statf[n * per_wide + b, 1:2, :] for b in range(per_wide)], axis=1
+                    )
+                    wg = nt_dot(vf[keys, :], gf[wide_of(n), :])
+                    for b in range(TALL // BLOCK):
+                        j = part * (TALL // BLOCK) + b
+                        ds = weights[n, block_of(j), :] * (
+                            wg[b * BLOCK : (b + 1) * BLOCK, :] - delta
+                        )
+                        colsum[n, pl.ds(j, 1), :] = jnp.sum(ds, axis=0, keepdims=True)
+                        low[n, block_of(j), :] = ds.astype(BF16)
+                return inner
+
+            return lax.fori_loop(0, wides // UNROLL, grad_step, carry)
+
+        lax.fori_loop(0, SIDE, part_step, 0)
         for i in range(genes):
             n, at = i // per_wide, i % per_wide * BLOCK
             sums = jnp.sum(colsum[n, :, at : at + BLOCK], axis=1, keepdims=True)
@@ -320,17 +365,16 @@
 
             @pl.when(step == 0)
             def _():
-                for to_step in range(1, genes):
+                for to_step in range(genes):
                     to = peer(to_step)[2]
                     pltpu.make_async_remote_copy(
                         src_ref=terms.at[to],
                         dst_ref=mine.at[head],
                         send_sem=term_send,
                         recv_sem=term_recv,
-                        device_id={"gene": to},
+                        device_id=device_at(to),
                         device_id_type=MESH,
                     ).start()
-                pltpu.make_async_copy(terms.at[gene], mine.at[head], term_recv).start()
 
             return carry
 
@@ -340,15 +384,13 @@
         def key_step(step, carry):
             m = wide_at(step)
             dk[wide_of(m), :] = (over_queries(m, qf) * scale).astype(BF16)
-
-            @pl.when(step > 0)
-            def _():
-                give_wide_back(1, dk, dk_out, step - 1)
-
             return carry
 
         lax.fori_loop(0, wides, key_step, 0)
-        give_wide_back(1, dk, dk_out, wides - 1)
+    @pl.when(jnp.logical_not(active))
+    def _():
+        pass_on(2, dv_out)
+        pass_on(0, dq_out)
 
     square[...] = jnp.zeros_like(square)
     arrived(mine, term_recv)
@@ -362,6 +404,25 @@
             device_id_type=MESH,
         ).start()
     pltpu.make_async_copy(mine, everyones.at[cell], cell_recv).start()
+
+    @pl.when(helped)
+    def _():
+        for k in range(near):
+            give_relay(1, dk, near_gene(k))
+
+    @pl.when(active)
+    def _():
+        for to in (0, 3, 4, 12, 1, 7, 8, 15, 2, 5, 11, 13, 6, 9, 14, 10):
+            direct = jnp.logical_not(jnp.logical_and(helped, place_near(to) < near))
+
+            @pl.when(direct)
+            def _():
+                give_direct(1, dk, dk_out, to)
+
+    @pl.when(jnp.logical_not(active))
+    def _():
+        pass_on(1, dk_out)
+
     arrived(everyones, cell_recv)
     everything = jnp.sum(everyones[...], axis=0)
     for h in range(heads):
@@ -377,20 +438,20 @@
         part = ref.at[pl.ds(0, count)]
         pltpu.make_async_copy(part, part, sem).wait()
 
+    for a in range(4):
+        sent(kf, heads * BLOCK, in_send.at[a])
+    sent(statf, heads, in_send.at[4])
+
     @pl.when(active)
     def _():
-        for a in range(4):
-            sent(kf, (heads - 1) * BLOCK, in_send.at[a])
-        sent(statf, heads - 1, in_send.at[4])
         for a in range(3):
-            sent(dq, (genes - 1) * BLOCK, out_send.at[a])
-        sent(terms, genes - 1, term_send)
+            sent(dq, genes * BLOCK, out_send.at[a])
+        sent(terms, genes, term_send)
 
     @pl.when(jnp.logical_not(active))
     def _():
-        for a in range(4):
-            sent(kf, heads * BLOCK, in_send.at[a])
-        sent(statf, heads, in_send.at[4])
+        for a in range(3):
+            sent(dq, near * BLOCK, out_send.at[a])
 
     if cells > 1:
         sent(everyones, cells - 1, cell_send)
@@ -455,6 +516,7 @@
             pltpu.VMEM((genes, 1, BLOCK), F32),
             pltpu.VMEM((heads, 1, BLOCK), F32),
             pltpu.VMEM((cells, heads, 1, BLOCK), F32),
+            pltpu.VMEM((3, 2 * SIDE * BLOCK, BLOCK), BF16),
             pltpu.VMEM((heads, 1, BLOCK), F32),
             pltpu.VMEM((heads, genes, genes), F32),
             pltpu.VMEM((genes, genes), jnp.int32),
@@ -462,6 +524,8 @@
             dma((6,)),
             dma((5,)),
             dma((5,)),
+            dma((SIDE,)),
+            dma((3,)),
             dma((3,)),
             dma((3,)),
             dma,

time: 80.1 us -> 75.5 us (0.943)
  Pallas kernels: 78.8 us -> 74.7 us
    pallas_call x1, Pallas kernels: 77.7 us -> 73.7 us  [shards(): pl.pallas_call(functools.partial(kernel, heads, genes, cells), out_shape=...]
where the time goes in v3:
time: 75.5 us; the launch traced here: 75.4 us
  Pallas kernels  74.7 us (99%)
    pallas_call x1, Pallas kernels, shards(): pl.pallas_call(functools.partial(kernel, heads, genes, cells), out_shape=...  73.7 us

profile of v3, /device:TPU:2, one launch (start us, length us, event | category | flops | bytes accessed | tf_op | source)
XLA Modules:
  0.0 75.4 jit_solution(14645794921077974541)
XLA Ops:
  0.6 73.7 %shard_map.120 = (bf16[1,128,1536]{2,1,0:T(8,128)(2,1)S(1)}, bf16[1,128,1536]{2,1,0:T(8,128)(2,1)S(1)}, bf16[1,128,1536]{2,1,0:T(8,128)(2,1)S(1)}, f32[1,1,12]{2,1,0:T(1,128)S(1)}) custom-call(bf16[1,128,1536]{2,1,0:T(8,128)(2,1)} %q_in.1, bf16[1,128,1536]{2,1,0:T(8,128)(2,1)} %k_in.1, bf16[1,128,1536]{2,1,0:T(8,128)(2,1)} %v_in.1, ...), custom_call_target="tpu_custom_call" | custom-call | tf_op jit(solution)/shard_map/pallas_call | solution.py:493
  74.3 1.0 %shard_map.121 = (bf16[1,128,1536]{2,1,0:T(8,128)(2,1)}, bf16[1,128,1536]{2,1,0:T(8,128)(2,1)}, bf16[1,128,1536]{2,1,0:T(8,128)(2,1)}, f32[1,1,12]{2,1,0:T(1,128)}) custom-call(bf16[1,128,1536]{2,1,0:T(8,128)(2,1)S(1)} %get-tuple-element.12.refs_0_, bf16[1,128,1536]{2,1,0:T(8,128)(2,1)S(1)} %get-tuple-element.13.refs_1_, ...), custom_call_target="tpu_custom_call" | custom-call | tf_op jit(solution)/shard_map/pallas_call | solution.py:550

commit v4 on v3

--- a/solution.py
+++ b/solution.py
@@ -14,6 +14,7 @@
 WIDE = 256
 TALL = 512
 UNROLL = 4
+RELAYED = 8
 LOG2E = 1.4426950408889634
 OFF = -1.0e30
 BF16 = jnp.bfloat16
@@ -108,8 +109,6 @@
     beside_cols = pl.ds(
         pl.multiple_of((live_heads * col + beside_place) * BLOCK, BLOCK), BLOCK
     )
-    way = 2 * half - 1
-    near = 2 * SIDE
 
     def peer(step):
         r, c = (row + step // SIDE) % SIDE, (col + step % SIDE) % SIDE
@@ -119,13 +118,16 @@
         return pl.ds(pl.multiple_of(i * BLOCK, BLOCK), BLOCK)
 
     barrier = pltpu.get_barrier_semaphore()
+    def alike(step):
+        return (cell // 4 + step // 2) % (cells // 4) * 4 + 2 * half + (core + step) % 2
+
     for step in range(genes):
-        pl.semaphore_signal(barrier, inc=1, device_id=device_at(peer(step)[2]), device_id_type=MESH)
-    pl.semaphore_signal(barrier, inc=1, device_id={"gene": beside}, device_id_type=MESH)
-    for step in range(1, cells):
-        pl.semaphore_signal(
-            barrier, inc=1, device_id={"cell": (cell + step) % cells}, device_id_type=MESH
-        )
+        to = peer(step)[2]
+        pl.semaphore_signal(barrier, inc=1, device_id=device_at(to), device_id_type=MESH)
+        if step > 0:
+            pl.semaphore_signal(barrier, inc=1, device_id={"gene": to}, device_id_type=MESH)
+    for step in range(1, cells // 2):
+        pl.semaphore_signal(barrier, inc=1, device_id={"cell": alike(step)}, device_id_type=MESH)
 
     loads = [
         pltpu.make_async_copy(src, dst, load_sem.at[n])
@@ -142,7 +144,7 @@
     ]
     for load in loads:
         load.start()
-    pl.semaphore_wait(barrier, genes + cells)
+    pl.semaphore_wait(barrier, 2 * genes + cells // 2 - 2)
 
     moved = ((k_in, kf), (q_in, qf), (g_in, gf), (v_in, vf))
 
@@ -212,57 +214,49 @@
             device_id_type=MESH,
         ).start()
 
-    def place_near(to):
-        return ((to % SIDE - col) * way + 2 * SIDE) % SIDE * SIDE + to // SIDE
-
-    def give_relay(a, src, to):
-        pltpu.make_async_remote_copy(
-            src_ref=src.at[block_of(to), :],
-            dst_ref=relay.at[a, block_of(place_near(to)), :],
-            send_sem=out_send.at[a],
-            recv_sem=relay_recv.at[a],
-            device_id={"gene": beside},
-            device_id_type=MESH,
-        ).start()
-
-    def near_gene(k):
-        return k % SIDE * SIDE + (col + k // SIDE * way + SIDE) % SIDE
-
-    def give_back(a, src, dst, to):
-        by_relay = jnp.logical_and(helped, place_near(to) < near)
-
-        @pl.when(by_relay)
-        def _():
-            give_relay(a, src, to)
-
-        @pl.when(jnp.logical_not(by_relay))
-        def _():
-            give_direct(a, src, dst, to)
-
-    def pass_on(a, dst):
-        arrived(relay.at[a], relay_recv.at[a])
-        for k in range(near):
+    wides = genes * BLOCK // WIDE
+    per_wide = WIDE // BLOCK
+
+    def wide_at(step):
+        return (gene // per_wide + step) % wides
+
+    def wide_of(n):
+        return pl.ds(pl.multiple_of(n * WIDE, WIDE), WIDE)
+
+    lap = RELAYED // per_wide
+
+    def give_wide_back(a, src, dst, step, relayed, stage):
+        for b in range(per_wide):
+            to = wide_at(step) * per_wide + b
+            by_relay = jnp.logical_and(helped, step < relayed)
+
+            @pl.when(by_relay)
+            def _():
+                pltpu.make_async_remote_copy(
+                    src_ref=src.at[block_of(to), :],
+                    dst_ref=relay.at[stage + step // lap, block_of(step % lap * per_wide + b), :],
+                    send_sem=out_send.at[a],
+                    recv_sem=relay_recv.at[stage + step // lap],
+                    device_id={"gene": beside},
+                    device_id_type=MESH,
+                ).start()
+
+            @pl.when(jnp.logical_not(by_relay))
+            def _():
+                give_direct(a, src, dst, to)
+
+    def pass_on(a, dst, stage, first):
+        arrived(relay.at[stage], relay_recv.at[stage])
+        for k in range(RELAYED):
+            m = (beside // per_wide + first + k // per_wide) % wides
             pltpu.make_async_remote_copy(
-                src_ref=relay.at[a, block_of(k), :],
+                src_ref=relay.at[stage, block_of(k), :],
                 dst_ref=dst.at[0, :, beside_cols],
                 send_sem=out_send.at[a],
                 recv_sem=out_recv.at[a],
-                device_id=device_at(near_gene(k)),
+                device_id=device_at(m * per_wide + k % per_wide),
                 device_id_type=MESH,
             ).start()
-
-    wides = genes * BLOCK // WIDE
-    per_wide = WIDE // BLOCK
-
-    def wide_at(step):
-        return (gene // per_wide + step) % wides
-
-    def wide_of(n):
-        return pl.ds(pl.multiple_of(n * WIDE, WIDE), WIDE)
-
-    def give_wide_back(a, src, dst, step):
-        for b in range(per_wide):
-            give_back(a, src, dst, wide_at(step) * per_wide + b)
 
     def over_queries(m, right):
         total = jnp.zeros((WIDE, BLOCK), F32)
@@ -319,12 +313,12 @@
 
             @pl.when(step > 0)
             def _():
-                give_wide_back(2, dv, dv_out, step - 1)
+                give_wide_back(2, dv, dv_out, step - 1, wides, 0)
 
             return carry
 
         lax.fori_loop(0, wides, value_step, 0)
-        give_wide_back(2, dv, dv_out, wides - 1)
+        give_wide_back(2, dv, dv_out, wides - 1, wides, 0)
 
         def part_step(k, carry):
             part = (row + SIDE - k) % SIDE
@@ -361,7 +355,7 @@
 
             @pl.when(step > 0)
             def _():
-                give_wide_back(0, dq, dq_out, step - 1)
+                give_wide_back(0, dq, dq_out, step - 1, lap, 2)
 
             @pl.when(step == 0)
             def _():
@@ -369,17 +363,27 @@
                     to = peer(to_step)[2]
                     pltpu.make_async_remote_copy(
                         src_ref=terms.at[to],
-                        dst_ref=mine.at[head],
-                        send_sem=term_send,
+                        dst_ref=mine.at[1 - half, head],
+                        send_sem=term_send.at[0],
                         recv_sem=term_recv,
                         device_id=device_at(to),
                         device_id_type=MESH,
                     ).start()
+                    if to_step > 0:
+                        pltpu.make_async_remote_copy(
+                            src_ref=terms.at[to],
+                            dst_ref=mine.at[1 - half, head],
+                            send_sem=term_send.at[1],
+                            recv_sem=term_recv,
+                            device_id={"gene": to},
+                            device_id_type=MESH,
+                        ).start()
+                pltpu.make_async_copy(terms.at[gene], mine.at[1 - half, head], term_recv).start()
 
             return carry
 
         lax.fori_loop(0, wides, query_step, 0)
-        give_wide_back(0, dq, dq_out, wides - 1)
+        give_wide_back(0, dq, dq_out, wides - 1, lap, 2)
 
         def key_step(step, carry):
             m = wide_at(step)
@@ -387,44 +391,32 @@
             return carry
 
         lax.fori_loop(0, wides, key_step, 0)
-    @pl.when(jnp.logical_not(active))
-    def _():
-        pass_on(2, dv_out)
-        pass_on(0, dq_out)
-
-    square[...] = jnp.zeros_like(square)
-    arrived(mine, term_recv)
-    for step in range(1, cells):
-        pltpu.make_async_remote_copy(
-            src_ref=mine,
-            dst_ref=everyones.at[cell],
-            send_sem=cell_send,
-            recv_sem=cell_recv,
-            device_id={"cell": (cell + step) % cells},
-            device_id_type=MESH,
-        ).start()
-    pltpu.make_async_copy(mine, everyones.at[cell], cell_recv).start()
-
-    @pl.when(helped)
-    def _():
-        for k in range(near):
-            give_relay(1, dk, near_gene(k))
-
     @pl.when(active)
     def _():
         for to in (0, 3, 4, 12, 1, 7, 8, 15, 2, 5, 11, 13, 6, 9, 14, 10):
-            direct = jnp.logical_not(jnp.logical_and(helped, place_near(to) < near))
-
-            @pl.when(direct)
-            def _():
-                give_direct(1, dk, dk_out, to)
+            give_direct(1, dk, dk_out, to)
 
     @pl.when(jnp.logical_not(active))
     def _():
-        pass_on(1, dk_out)
-
+        pass_on(2, dv_out, 0, 0)
+        pass_on(2, dv_out, 1, lap)
+        pass_on(0, dq_out, 2, 0)
+
+    square[...] = jnp.zeros_like(square)
+    arrived(mine, term_recv)
+    own_place = cell // 4 * 2 + core
+    for step in range(1, cells // 2):
+        pltpu.make_async_remote_copy(
+            src_ref=mine,
+            dst_ref=everyones.at[own_place],
+            send_sem=cell_send,
+            recv_sem=cell_recv,
+            device_id={"cell": alike(step)},
+            device_id_type=MESH,
+        ).start()
+    pltpu.make_async_copy(mine, everyones.at[own_place], cell_recv).start()
     arrived(everyones, cell_recv)
-    everything = jnp.sum(everyones[...], axis=0)
+    everything = jnp.sum(everyones[...], axis=(0, 1))
     for h in range(heads):
         square[h : h + 1, :] = everything[h]
     slot_rows = lax.broadcasted_iota(jnp.int32, (BLOCK, BLOCK), 0)
@@ -446,15 +438,15 @@
     def _():
         for a in range(3):
             sent(dq, genes * BLOCK, out_send.at[a])
-        sent(terms, genes, term_send)
+        sent(terms, genes, term_send.at[0])
+        sent(terms, genes - 1, term_send.at[1])
 
     @pl.when(jnp.logical_not(active))
     def _():
-        for a in range(3):
-            sent(dq, near * BLOCK, out_send.at[a])
-
-    if cells > 1:
-        sent(everyones, cells - 1, cell_send)
+        sent(dv, genes * BLOCK, out_send.at[2])
+        sent(dq, RELAYED * BLOCK, out_send.at[0])
+
+    sent(everyones, cells // 2 - 1, cell_send)
 
 
 def put_out(*refs):
@@ -514,9 +506,9 @@
             pltpu.VMEM((rows, BLOCK), BF16),
             pltpu.VMEM((rows, BLOCK), BF16),
             pltpu.VMEM((genes, 1, BLOCK), F32),
-            pltpu.VMEM((heads, 1, BLOCK), F32),
-            pltpu.VMEM((cells, heads, 1, BLOCK), F32),
-            pltpu.VMEM((3, 2 * SIDE * BLOCK, BLOCK), BF16),
+            pltpu.VMEM((2, heads, 1, BLOCK), F32),
+            pltpu.VMEM((cells // 2, 2, heads, 1, BLOCK), F32),
+            pltpu.VMEM((3, RELAYED * BLOCK, BLOCK), BF16),
             pltpu.VMEM((heads, 1, BLOCK), F32),
             pltpu.VMEM((heads, genes, genes), F32),
             pltpu.VMEM((genes, genes), jnp.int32),
@@ -528,7 +520,7 @@
             dma((3,)),
             dma((3,)),
             dma((3,)),
-            dma,
+            dma((2,)),
             dma,
             dma,
             dma,

time: 75.5 us -> 74.3 us (0.984)
  Pallas kernels: 74.7 us -> 72.8 us
    pallas_call x1, Pallas kernels: 73.7 us -> 71.8 us  [shards(): pl.pallas_call(functools.partial(kernel, heads, genes, cells), out_shape=...]
where the time goes in v4:
time: 74.3 us; the launch traced here: 73.5 us
  Pallas kernels  72.8 us (98%)
    pallas_call x1, Pallas kernels, shards(): pl.pallas_call(functools.partial(kernel, heads, genes, cells), out_shape=...  71.8 us

profile of v4, /device:TPU:2, one launch (start us, length us, event | category | flops | bytes accessed | tf_op | source)
XLA Modules:
  0.0 73.5 jit_solution(7633548989261634531)
XLA Ops:
  0.6 71.8 %shard_map.120 = (bf16[1,128,1536]{2,1,0:T(8,128)(2,1)S(1)}, bf16[1,128,1536]{2,1,0:T(8,128)(2,1)S(1)}, bf16[1,128,1536]{2,1,0:T(8,128)(2,1)S(1)}, f32[1,1,12]{2,1,0:T(1,128)S(1)}) custom-call(bf16[1,128,1536]{2,1,0:T(8,128)(2,1)} %q_in.1, bf16[1,128,1536]{2,1,0:T(8,128)(2,1)} %k_in.1, bf16[1,128,1536]{2,1,0:T(8,128)(2,1)} %v_in.1, ...), custom_call_target="tpu_custom_call" | custom-call | tf_op jit(solution)/shard_map/pallas_call | solution.py:485
  72.4 1.0 %shard_map.121 = (bf16[1,128,1536]{2,1,0:T(8,128)(2,1)}, bf16[1,128,1536]{2,1,0:T(8,128)(2,1)}, bf16[1,128,1536]{2,1,0:T(8,128)(2,1)}, f32[1,1,12]{2,1,0:T(1,128)}) custom-call(bf16[1,128,1536]{2,1,0:T(8,128)(2,1)S(1)} %get-tuple-element.12.refs_0_, bf16[1,128,1536]{2,1,0:T(8,128)(2,1)S(1)} %get-tuple-element.13.refs_1_, ...), custom_call_target="tpu_custom_call" | custom-call | tf_op jit(solution)/shard_map/pallas_call | solution.py:542

commit v5 on v4

--- a/solution.py
+++ b/solution.py
@@ -14,7 +14,7 @@
 WIDE = 256
 TALL = 512
 UNROLL = 4
-RELAYED = 8
+RELAYED = 4
 LOG2E = 1.4426950408889634
 OFF = -1.0e30
 BF16 = jnp.bfloat16
@@ -87,6 +87,7 @@
     cell = lax.axis_index("cell")
     row, col = gene // SIDE, gene % SIDE
     core, half = cell % 2, (cell // 2) % 2
+    way = 2 * half - 1
     other = cell + 2 - 4 * half
     live_heads = heads // SIDE
     scale = 1.0 / math.sqrt(BLOCK)
@@ -121,10 +122,18 @@
     def alike(step):
         return (cell // 4 + step // 2) % (cells // 4) * 4 + 2 * half + (core + step) % 2
 
-    for step in range(genes):
-        to = peer(step)[2]
-        pl.semaphore_signal(barrier, inc=1, device_id=device_at(to), device_id_type=MESH)
-        if step > 0:
+    def hops(entry):
+        theirs, down, over = entry
+        along = (1, 1, 3, 3)[over] if theirs else (0, 2, 4, 2)[over]
+        return min(down, SIDE - down) + along
+
+    greeted = [(t, d, e) for t in (True, False) for d in range(SIDE) for e in range(SIDE)]
+    for theirs, down, over in sorted(greeted, key=hops, reverse=True):
+        r, c = (row + down) % SIDE, (col + over * way + SIDE) % SIDE
+        to = r * SIDE + c
+        if theirs:
+            pl.semaphore_signal(barrier, inc=1, device_id=device_at(to), device_id_type=MESH)
+        elif down + over > 0:
             pl.semaphore_signal(barrier, inc=1, device_id={"gene": to}, device_id_type=MESH)
     for step in range(1, cells // 2):
         pl.semaphore_signal(barrier, inc=1, device_id={"cell": alike(step)}, device_id_type=MESH)
@@ -225,6 +234,13 @@
 
     lap = RELAYED // per_wide
 
+    def early_at(step):
+        return lax.shift_right_logical(jnp.int32(16096528), jnp.int32(3) * step) % wides
+
+    def give_keys(step):
+        for b in range(per_wide):
+            give_direct(1, dk, dk_out, early_at(step) * per_wide + b)
+
     def give_wide_back(a, src, dst, step, relayed, stage):
         for b in range(per_wide):
             to = wide_at(step) * per_wide + b
@@ -355,7 +371,7 @@
 
             @pl.when(step > 0)
             def _():
-                give_wide_back(0, dq, dq_out, step - 1, lap, 2)
+                give_wide_back(0, dq, dq_out, step - 1, wides // 2, 4)
 
             @pl.when(step == 0)
             def _():
@@ -383,24 +399,26 @@
             return carry
 
         lax.fori_loop(0, wides, query_step, 0)
-        give_wide_back(0, dq, dq_out, wides - 1, lap, 2)
+        give_wide_back(0, dq, dq_out, wides - 1, wides // 2, 4)
 
         def key_step(step, carry):
-            m = wide_at(step)
+            m = early_at(step)
             dk[wide_of(m), :] = (over_queries(m, qf) * scale).astype(BF16)
+
+            @pl.when(step > 0)
+            def _():
+                give_keys(step - 1)
+
             return carry
 
         lax.fori_loop(0, wides, key_step, 0)
-    @pl.when(active)
-    def _():
-        for to in (0, 3, 4, 12, 1, 7, 8, 15, 2, 5, 11, 13, 6, 9, 14, 10):
-            give_direct(1, dk, dk_out, to)
-
+        give_keys(wides - 1)
     @pl.when(jnp.logical_not(active))
     def _():
-        pass_on(2, dv_out, 0, 0)
-        pass_on(2, dv_out, 1, lap)
-        pass_on(0, dq_out, 2, 0)
+        for part in range(4):
+            pass_on(2, dv_out, part, part * lap)
+        for part in range(2):
+            pass_on(0, dq_out, 4 + part, part * lap)
 
     square[...] = jnp.zeros_like(square)
     arrived(mine, term_recv)
@@ -444,7 +462,7 @@
     @pl.when(jnp.logical_not(active))
     def _():
         sent(dv, genes * BLOCK, out_send.at[2])
-        sent(dq, RELAYED * BLOCK, out_send.at[0])
+        sent(dq, genes // 2 * BLOCK, out_send.at[0])
 
     sent(everyones, cells // 2 - 1, cell_send)
 
@@ -508,7 +526,7 @@
             pltpu.VMEM((genes, 1, BLOCK), F32),
             pltpu.VMEM((2, heads, 1, BLOCK), F32),
             pltpu.VMEM((cells // 2, 2, heads, 1, BLOCK), F32),
-            pltpu.VMEM((3, RELAYED * BLOCK, BLOCK), BF16),
+            pltpu.VMEM((6, RELAYED * BLOCK, BLOCK), BF16),
             pltpu.VMEM((heads, 1, BLOCK), F32),
             pltpu.VMEM((heads, genes, genes), F32),
             pltpu.VMEM((genes, genes), jnp.int32),
@@ -519,7 +537,7 @@
             dma((SIDE,)),
             dma((3,)),
             dma((3,)),
-            dma((3,)),
+            dma((6,)),
             dma((2,)),
             dma,
             dma,

time: 74.3 us -> 74 us (level)
  Pallas kernels: 72.8 us -> 71.9 us
    pallas_call x1, Pallas kernels: 71.8 us -> 70.9 us  [shards(): pl.pallas_call(functools.partial(kernel, heads, genes, cells), out_shape=...]
where the time goes in v5:
time: 74 us; the launch traced here: 72.6 us
  Pallas kernels  71.9 us (97%)
    pallas_call x1, Pallas kernels, shards(): pl.pallas_call(functools.partial(kernel, heads, genes, cells), out_shape=...  70.9 us

profile of v5, /device:TPU:2, one launch (start us, length us, event | category | flops | bytes accessed | tf_op | source)
XLA Modules:
  0.0 72.6 jit_solution(2982424045133212256)
XLA Ops:
  0.6 70.9 %shard_map.120 = (bf16[1,128,1536]{2,1,0:T(8,128)(2,1)S(1)}, bf16[1,128,1536]{2,1,0:T(8,128)(2,1)S(1)}, bf16[1,128,1536]{2,1,0:T(8,128)(2,1)S(1)}, f32[1,1,12]{2,1,0:T(1,128)S(1)}) custom-call(bf16[1,128,1536]{2,1,0:T(8,128)(2,1)} %q_in.1, bf16[1,128,1536]{2,1,0:T(8,128)(2,1)} %k_in.1, bf16[1,128,1536]{2,1,0:T(8,128)(2,1)} %v_in.1, ...), custom_call_target="tpu_custom_call" | custom-call | tf_op jit(solution)/shard_map/pallas_call | solution.py:503
  71.5 1.0 %shard_map.121 = (bf16[1,128,1536]{2,1,0:T(8,128)(2,1)}, bf16[1,128,1536]{2,1,0:T(8,128)(2,1)}, bf16[1,128,1536]{2,1,0:T(8,128)(2,1)}, f32[1,1,12]{2,1,0:T(1,128)}) custom-call(bf16[1,128,1536]{2,1,0:T(8,128)(2,1)S(1)} %get-tuple-element.12.refs_0_, bf16[1,128,1536]{2,1,0:T(8,128)(2,1)S(1)} %get-tuple-element.13.refs_1_, ...), custom_call_target="tpu_custom_call" | custom-call | tf_op jit(solution)/shard_map/pallas_call | solution.py:560

commit v6 on v5

--- a/solution.py
+++ b/solution.py
@@ -158,8 +158,12 @@
     moved = ((k_in, kf), (q_in, qf), (g_in, gf), (v_in, vf))
 
     def send_array(a, src, dst, recv_sem):
-        for step in range(genes):
-            r, c, to = peer(step)
+        for k in range(genes):
+            down, e = k // 2 % SIDE, k // (2 * SIDE) * 2 + k % 2
+            if src is v_in:
+                down, e = k // SIDE, k % SIDE
+            r, c = (row + down) % SIDE, (col + e * way + SIDE) % SIDE
+            to = r * SIDE + c
             spot = slot_of(r, 1 - half)
 
             @pl.when(spot < live_heads)

time: 74 us -> 74 us (level)
  no operation moved by 1% of the time
where the time goes in v6:
time: 74 us; the launch traced here: 72.6 us
  Pallas kernels  72 us (97%)
    pallas_call x1, Pallas kernels, shards(): pl.pallas_call(functools.partial(kernel, heads, genes, cells), out_shape=...  71 us

profile of v6, /device:TPU:2, one launch (start us, length us, event | category | flops | bytes accessed | tf_op | source)
XLA Modules:
  0.0 72.6 jit_solution(14738934189871785183)
XLA Ops:
  0.6 71.0 %shard_map.120 = (bf16[1,128,1536]{2,1,0:T(8,128)(2,1)S(1)}, bf16[1,128,1536]{2,1,0:T(8,128)(2,1)S(1)}, bf16[1,128,1536]{2,1,0:T(8,128)(2,1)S(1)}, f32[1,1,12]{2,1,0:T(1,128)S(1)}) custom-call(bf16[1,128,1536]{2,1,0:T(8,128)(2,1)} %q_in.1, bf16[1,128,1536]{2,1,0:T(8,128)(2,1)} %k_in.1, bf16[1,128,1536]{2,1,0:T(8,128)(2,1)} %v_in.1, ...), custom_call_target="tpu_custom_call" | custom-call | tf_op jit(solution)/shard_map/pallas_call | solution.py:507
  71.6 1.0 %shard_map.121 = (bf16[1,128,1536]{2,1,0:T(8,128)(2,1)}, bf16[1,128,1536]{2,1,0:T(8,128)(2,1)}, bf16[1,128,1536]{2,1,0:T(8,128)(2,1)}, f32[1,1,12]{2,1,0:T(1,128)}) custom-call(bf16[1,128,1536]{2,1,0:T(8,128)(2,1)S(1)} %get-tuple-element.12.refs_0_, bf16[1,128,1536]{2,1,0:T(8,128)(2,1)S(1)} %get-tuple-element.13.refs_1_, ...), custom_call_target="tpu_custom_call" | custom-call | tf_op jit(solution)/shard_map/pallas_call | solution.py:564
